TPU v7x, 32 devices: a whole 2x2x4 slice. The times are simulated.
32 devices in a mesh: gx: 4 (over y, x), gy: 8 (over z, core).
Axes of the slice: x: 2, y: 2, z: 4, core: 2. Of those that a mesh axis runs over, the one named last changes fastest.
Arguments:
- potential: float32 [16, 256, 1024], P(None, 'gx', 'gy'), may hold values from -4 to 4
- labels: int32 [16, 256, 1024], P(None, 'gx', 'gy'), may hold values from 0 to 2, as said below
- voltages: float32 [2], replicated, may hold values from -3 to 3
- ion_blocks: bfloat16 [32, 32, 4096], P(('gx', 'gy')), may hold values from 0.19921875 to 2
- owner_map: int32 [32, 32], P(None, ('gx', 'gy')), may hold values from 0 to 31, as said below
Outputs:
- potential_next: float32 [16, 256, 1024], P(None, 'gx', 'gy')
Inputs may be any that keep to these rules, and one draw needn't show every extreme that they name: `labels`: 0 marks plasma cells, 1 the screen electrode and 2 the accelerator electrode; the electrodes are plates of a few planes pierced by round apertures every 51 cells. For every brick k, the column owner_map[:, k] names each block index of brick k exactly once.
All inputs are finite; a program needn't handle non-finite values.
Results may differ from a plain program's by a relative error of at most 0.0003.
Values may be sent and summed in bfloat16 or wider, within the bound.
No kernel may reach another device: no remote copies, remote signals or barrier semaphores. Data moves between devices by JAX's collectives and lax.ppermute only.
A program may use at most 64 MiB of HBM per device.

v0:
```python
import functools

import jax
import jax.numpy as jnp
from jax import lax
from jax.experimental import pallas as pl
from jax.experimental.pallas import tpu as pltpu
from jax.sharding import PartitionSpec as P

HALO = 12
LOW = 32
HIGH = 64

debye_term = 1.0
damping = 0.5

f32 = jnp.float32
bf16 = jnp.bfloat16


def lane_iota(rows):
    return lax.broadcasted_iota(jnp.int32, (rows, 128), 1)


def between(lane, low, high):
    return (lane >= low) & (lane < high)


def roll(value, shift):
    shift = shift % 128
    return value if shift == 0 else pltpu.roll(value, shift, 1)


def x_pack_kernel(nz, rx, pot, lab, own_map, up, down):
    def row(ref, x):
        return ref[pl.ds(x, nz, stride=rx), :]

    for out, first, near in ((up, 0, 0), (down, rx - HALO, rx - 4)):
        for i in range(HALO):
            value = row(pot, first + i)
            high = value.astype(bf16)
            out[i] = high
            offset = first + i - near
            if 0 <= offset < 4:
                out[HALO + offset] = (value - high.astype(f32)).astype(bf16)
            out[HALO + 4 + i] = (row(lab, first + i) + 1).astype(f32).astype(bf16)
        out[2 * HALO + 4] = own_map[...].astype(bf16)


def y_pack_kernel(nz, rx, pot, lab, own_map, before, after, pa, la, left, right):
    wide = rx + 2 * HALO
    for i in range(HALO):
        value = before[i].astype(f32)
        if i >= HALO - 4:
            value = value + before[HALO + i - (HALO - 4)].astype(f32)
        pa[i] = value
        la[i] = before[HALO + 4 + i].astype(f32)
        value = after[i].astype(f32)
        if i < 4:
            value = value + after[HALO + i].astype(f32)
        pa[HALO + rx + i] = value
        la[HALO + rx + i] = after[HALO + 4 + i].astype(f32)

    def copy_rows(step, carry):
        for q in range(4):
            x = step * 4 + q
            pa[HALO + x] = pot[pl.ds(x, nz, stride=rx), :]
            la[HALO + x] = (lab[pl.ds(x, nz, stride=rx), :] + 1).astype(f32)
        return carry

    lax.fori_loop(0, rx // 4, copy_rows, 0)

    lane = lane_iota(nz)
    is_low = between(lane, 12, 16)
    is_label = lane >= 16
    group_of = lane // 32

    def group(g, carry):
        to_left = jnp.zeros((nz, 128), f32)
        to_right = jnp.zeros((nz, 128), f32)
        for q in range(4):
            value = pa[g * 4 + q]
            code = la[g * 4 + q]
            high = value.astype(bf16).astype(f32)
            low = value - high
            one = jnp.where(is_label, roll(code, 16), jnp.where(is_low, roll(low, 12), high))
            two = jnp.where(is_label, roll(code, 28), jnp.where(is_low, roll(low, 16), roll(high, 12)))
            here = group_of == q
            to_left = jnp.where(here, roll(one, 32 * q), to_left)
            to_right = jnp.where(here, roll(two, 32 * q), to_right)
        left[g] = to_left.astype(bf16)
        right[g] = to_right.astype(bf16)
        return carry

    lax.fori_loop(0, wide // 4, group, 0)
    row = lax.broadcasted_iota(jnp.int32, (nz, 128), 0)
    maps = jnp.where(
        row == 0,
        before[2 * HALO + 4].astype(f32),
        jnp.where(row == 1, own_map[...], after[2 * HALO + 4].astype(f32)),
    ).astype(bf16)
    left[wide // 4] = maps
    right[wide // 4] = maps


def neighbour_rows(ref_a, ref_b, i, nz, lane, low_row, high_row):
    a = ref_a[i, pl.ds(8, nz), :]
    b = ref_b[i, pl.ds(8, nz), :]
    first = lane == 0
    last = lane == 127
    ra, rb = roll(a, 1), roll(b, 1)
    la, lb = roll(a, 127), roll(b, 127)
    out_a = jnp.where(first, rb, ra) + jnp.where(last, lb, la)
    out_b = jnp.where(first, ra, rb) + jnp.where(last, la, lb)
    out_a = out_a + ref_a[i, pl.ds(7, nz), :] + ref_a[i, pl.ds(9, nz), :]
    out_b = out_b + ref_b[i, pl.ds(7, nz), :] + ref_b[i, pl.ds(9, nz), :]
    for beside in (low_row, high_row):
        if beside is not None:
            out_a = out_a + beside[0]
            out_b = out_b + beside[1]
    return out_a, out_b


def read_row(ref_a, ref_b, i, nz):
    return ref_a[i, pl.ds(8, nz), :], ref_b[i, pl.ds(8, nz), :]


def clear_pads(refs, count, nz):
    zero = jnp.zeros((8, 128), f32)

    def body(i, carry):
        for ref in refs:
            ref[i, pl.ds(0, 8), :] = zero
            ref[i, pl.ds(8 + nz, 8), :] = zero
        return carry

    lax.fori_loop(0, count, body, 0)


def spread(lane, left_right, a, q):
    base = roll(left_right, -32 * q)
    out = jnp.where(between(lane, 20, 32), roll(base, 20), jnp.zeros_like(base))
    out = jnp.where(between(lane, 119, 128), roll(base, 116), out)
    out = jnp.where(between(lane, 0, 9), roll(base, -16), out)
    out = jnp.where(between(lane, 64, 76), roll(base, 48), out)
    out = jnp.where(between(lane, 32, 41), roll(a, LOW), out)
    return jnp.where(between(lane, 55, 64), roll(a, HIGH), out)


def absent_lanes(lane):
    index = lax.axis_index("gy")
    none_before = between(lane, 20, 41) & (index == 0)
    none_after = between(lane, 55, 76) & (index == lax.axis_size("gy") - 1)
    return none_before | none_after


def weight_kernel(nz, rx, volts, pa, la, from_left, from_right, own_side, wa, wb, ca, cb, maps, ppa, ppb, lbb):
    wide = rx + 2 * HALO
    lane = lane_iota(nz)
    within = lane % 32
    clear_pads((ppa, ppb), wide, nz)

    def unpack(g, carry):
        tl = from_left[g].astype(f32)
        tr = from_right[g].astype(f32)
        pot_l = tl + jnp.where(between(within, 8, 12), roll(tl, -4), 0.0)
        pot_r = tr + jnp.where(within < 4, roll(tr, -12), 0.0)
        pot_lr = jnp.where(within < 12, pot_l, roll(pot_r, 16))
        lab_lr = jnp.where(within < 12, roll(tl, -16), tr)
        for q in range(4):
            i = g * 4 + q
            a = pa[i]
            ppa[i, pl.ds(8, nz), :] = a
            ppb[i, pl.ds(8, nz), :] = spread(lane, pot_lr, a, q)
            lbb[i] = spread(lane, lab_lr, la[i], q)
        return carry

    lax.fori_loop(0, wide // 4, unpack, 0)
    kept = between(lane, 0, 8) | between(lane, 21, 40) | between(lane, 56, 75) | between(lane, 120, 128)
    kept = kept & ~absent_lanes(lane)
    v0 = volts[0]
    v1 = volts[1]

    def rows(i, carry):
        n_a, n_b = neighbour_rows(
            ppa, ppb, i, nz, lane, read_row(ppa, ppb, i - 1, nz), read_row(ppa, ppb, i + 1, nz)
        )
        p_a, p_b = read_row(ppa, ppb, i, nz)
        for p, n, code, w_out, c_out, mask in (
            (p_a, n_a, la[i], wa, ca, None),
            (p_b, n_b, lbb[i], wb, cb, kept),
        ):
            growth = jnp.exp(p)
            inverse = 1.0 / (6.0 + debye_term * growth)
            plasma = between(code, 0.5, 1.5)
            edge = jnp.where(code < 2.5, v0, v1)
            inside = code > 0.5
            if mask is not None:
                plasma = plasma & mask
                inside = inside & mask
            w = jnp.where(plasma, (n - 6.0 * p - debye_term * growth) * inverse, edge - p)
            w_out[i] = jnp.where(inside, w, 0.0)
            c_out[i] = jnp.where(plasma, inverse, 0.0)
        return carry

    lax.fori_loop(1, wide - 1, rows, 0)
    zero = jnp.zeros((nz, 128), f32)
    for i in (0, wide - 1):
        for ref in (wa, wb, ca, cb):
            ref[i] = zero
    maps[pl.ds(0, 8), :] = from_left[wide // 4].astype(f32)[0:8].astype(jnp.int32)
    maps[pl.ds(8, 8), :] = own_side[wide // 4].astype(f32)[0:8].astype(jnp.int32)
    maps[pl.ds(16, 8), :] = from_right[wide // 4].astype(f32)[0:8].astype(jnp.int32)


def slot_kernel(count, ny, tiles, blocks, out, field):
    rows = tiles * 8
    for r in range(rows):
        field[pl.ds(r, count, stride=rows), :] = blocks[:, pl.ds(r * 128, 128)].astype(f32)
    lane = lane_iota(8)
    sub = lax.broadcasted_iota(jnp.int32, (8, 128), 0)

    def one(k, carry):
        def tile(offset, t):
            brick = lax.rem(k + offset + count, count)
            return field[pl.ds(pl.multiple_of(brick * rows + t * 8, 8), 8), :]

        parts = [tile(0, t) for t in range(tiles)]
        if tiles == 1:
            parts += [tile(ny, 0), tile(-ny, 0)]
        else:
            mixed = jnp.where(sub < 4, tile(ny, 1), tile(-ny, tiles - 2))
            parts += [tile(ny, 0), mixed, tile(-ny, tiles - 1)]

        def pair(offset, t, at):
            low = roll(tile(offset - 1, t), 12 + at)
            high = roll(tile(offset + 1, t), 16 + at)
            return jnp.where(between(lane, at, at + 12), low, high)

        sides = jnp.zeros((8, 128), f32)
        for t in range(tiles):
            sides = jnp.where(between(lane, 32 * t, 32 * t + 32), pair(0, t, 32 * t), sides)
        corners = jnp.where(lane < 32, pair(ny, 0, 0), pair(-ny, tiles - 1, 32))
        if tiles > 1:
            second = jnp.where(lane < 96, pair(ny, 1, 64), pair(-ny, tiles - 2, 96))
            corners = jnp.where(lane < 64, corners, second)
        parts += [sides, corners]
        out[k] = jnp.concatenate(parts, axis=0).astype(bf16)
        return carry

    lax.fori_loop(0, count, one, 0)


def sweep_kernel(nz, rx, count, tiles, maps, got, wa, wb, ca, cb, pot, out, *scratch):
    (ra, rb, xa, xb, ya, yb, ua, ub, cut_a, cut_b, ch_a, ch_l, ch_r, va, vb) = scratch
    wide = rx + 2 * HALO
    tall = rx + 32
    per_plane = rx // (8 * tiles)
    lane = lane_iota(nz)
    lane8 = lane_iota(8)
    clear_pads((ra, rb, xa, xb, ya, yb, ua, ub), wide, nz)
    clear_pads((cut_a, cut_b), cut_a.shape[0], nz)

    def place(p, carry):
        slot = got[p].astype(f32)
        pieces = [slot[8 * t : 8 * t + 8] for t in range(slot.shape[0] // 8)]

        def where_to(which, side):
            index = maps[which, p]
            z = index // per_plane
            part = index - z * per_plane
            if side == 0:
                return z, part, None
            depth = part if side > 0 else per_plane - 1 - part
            ok = depth * 8 * tiles < HALO
            return jnp.where(ok, z, nz), part, jnp.where(ok, depth, 0)

        def put(ref, z, row, value):
            ref[pl.ds(pl.multiple_of(z * tall + row, 8), 8), :] = value

        z, part, _ = where_to(9, 0)
        for t in range(tiles):
            put(ch_a, z, 16 + (part * tiles + t) * 8, pieces[t])
        zp, _, dp = where_to(10, 1)
        zm, _, dm = where_to(8, -1)
        if tiles == 1:
            put(ch_a, zp, 16 + rx + dp * 8, pieces[1])
            put(ch_a, zm, 8 - dm * 8, pieces[2])
            next_piece = 3
        else:
            put(ch_a, zp, 16 + rx, pieces[tiles])
            put(ch_a, zp, 24 + rx, pieces[tiles + 1])
            put(ch_a, zm, 0, pieces[tiles + 1])
            put(ch_a, zm, 8, pieces[tiles + 2])
            next_piece = tiles + 3
        sides = pieces[next_piece]
        corners = pieces[next_piece + 1]
        zl, part_l, _ = where_to(1, 0)
        zr, part_r, _ = where_to(17, 0)
        for t in range(tiles):
            value = roll(sides, -32 * t)
            put(ch_l, zl, 16 + (part_l * tiles + t) * 8, value)
            put(ch_r, zr, 16 + (part_r * tiles + t) * 8, value)
        for which, side, at, ref in ((2, 1, 0, ch_l), (18, 1, 0, ch_r), (0, -1, 32, ch_l), (16, -1, 32, ch_r)):
            z, _, depth = where_to(which, side)
            value = roll(corners, -at)
            if tiles == 1:
                put(ref, z, (16 + rx + depth * 8) if side > 0 else (8 - depth * 8), value)
            else:
                put(ref, z, (16 + rx) if side > 0 else 8, value)
                put(ref, z, (24 + rx) if side > 0 else 0, roll(corners, -at - 64))
        return carry

    lax.fori_loop(0, count, place, 0)

    def weights(i, carry):
        x = i + 4
        a = ch_a[pl.ds(x, nz, stride=tall), :]
        low = ch_l[pl.ds(x, nz, stride=tall), :]
        high = ch_r[pl.ds(x, nz, stride=tall), :]
        b = jnp.where(between(lane, 20, 32), roll(low, 20), 0.0)
        b = jnp.where(between(lane, 119, 128), roll(low, 116), b)
        b = jnp.where(between(lane, 0, 9), roll(high, -16), b)
        b = jnp.where(between(lane, 64, 76), roll(high, 48), b)
        b = jnp.where(between(lane, 32, 41), roll(a, LOW), b)
        b = jnp.where(between(lane, 55, 64), roll(a, HIGH), b)
        w_a = wa[i] + jnp.where(ca[i] > 0.0, debye_term * ca[i] * a, 0.0)
        w_b = wb[i] + jnp.where(cb[i] > 0.0, debye_term * cb[i] * b, 0.0)
        va[i] = w_a
        vb[i] = w_b
        ra[i, pl.ds(8, nz), :] = w_a
        rb[i, pl.ds(8, nz), :] = w_b
        return carry

    lax.fori_loop(1, wide - 1, weights, 0)

    def iterate(src, dst, low, high):
        def body(step, carry):
            i = low + step * 2
            rows = [read_row(*src, i + d, nz) for d in (-1, 0, 1, 2)]
            for d in (0, 1):
                n_a, n_b = neighbour_rows(*src, i + d, nz, lane, rows[d], rows[d + 2])
                dst[0][i + d, pl.ds(8, nz), :] = ra[i + d, pl.ds(8, nz), :] + ca[i + d] * n_a
                dst[1][i + d, pl.ds(8, nz), :] = rb[i + d, pl.ds(8, nz), :] + cb[i + d] * n_b
            return carry

        lax.fori_loop(0, (high - low) // 2, body, 0)

    def cut(level, at, edge, step):
        sources = {2: (ra, rb), 3: (xa, xb), 4: (ya, yb)}
        starts = {2: 0, 3: 1, 4: 3}
        whole = sources[level]
        for j in range(level - 1):
            i = edge + step * j
            if j < level - 2:
                own_refs, own_i = (cut_a, cut_b), at + starts[level - 1] + j
            else:
                own_refs, own_i = whole, i
            if j == 0:
                inner_out = None
            else:
                inner_out = read_row(cut_a, cut_b, at + starts[level - 1] + j - 1, nz)
            if j + 1 < level - 2:
                inner_in = read_row(cut_a, cut_b, at + starts[level - 1] + j + 1, nz)
            else:
                inner_in = read_row(*whole, i + step, nz)
            n_a, n_b = neighbour_rows(*own_refs, own_i, nz, lane, inner_out, inner_in)
            slot = at + starts[level] + j
            cut_a[slot, pl.ds(8, nz), :] = ra[i, pl.ds(8, nz), :] + ca[i] * n_a
            cut_b[slot, pl.ds(8, nz), :] = rb[i, pl.ds(8, nz), :] + cb[i] * n_b

    mid_low = HALO + 7
    mid_high = HALO + rx - 8
    end_low = HALO - 8
    end_high = HALO + rx + 7

    def combined(a, b):
        b_high = roll(b, HIGH)
        b_low = roll(b, -LOW)
        new_a = a + jnp.where(lane < 8, b_low, jnp.where(lane >= 120, b_high, 0.0))
        more = jnp.where(between(lane, 32, 41), roll(a, LOW), 0.0)
        more = jnp.where(between(lane, 55, 64), roll(a, HIGH), more)
        more = jnp.where((lane < 8) | between(lane, 64, 72), b_high, more)
        more = jnp.where(between(lane, 24, 32), roll(b, LOW), more)
        more = jnp.where(lane >= 120, b_low, more)
        return new_a, b + more

    ghost = (lane == 40) | (lane == 55) | absent_lanes(lane)
    index = lax.axis_index("gx")
    has_low = jnp.where(index > 0, 1.0, 0.0)
    has_high = jnp.where(index < lax.axis_size("gx") - 1, 1.0, 0.0)
    lowest = 1
    for sweep in range(3):
        last = sweep == 2
        if sweep > 0:
            lowest = lowest + 4

            def residual(step, carry):
                i = lowest + step * 2
                rows = [read_row(ua, ub, i + d, nz) for d in (-1, 0, 1, 2)]
                for d in (0, 1):
                    n_a, n_b = neighbour_rows(ua, ub, i + d, nz, lane, rows[d], rows[d + 2])
                    r_a = va[i + d] - rows[d + 1][0] + ca[i + d] * n_a
                    r_b = vb[i + d] - rows[d + 1][1] + cb[i + d] * n_b
                    ra[i + d, pl.ds(8, nz), :] = r_a
                    rb[i + d, pl.ds(8, nz), :] = jnp.where(ghost, 0.0, r_b)
                return carry

            lax.fori_loop(0, (wide - 2 * lowest) // 2, residual, 0)
        iterate((ra, rb), (xa, xb), lowest + 1, wide - lowest - 1)
        iterate((xa, xb), (ya, yb), lowest + 2, wide - lowest - 2)
        ends = [(0, mid_low, -1), (6, mid_high, 1)]
        if sweep == 0:
            ends += [(12, end_low, 1), (18, end_high, -1)]
        for at, edge, step in ends:
            for level in (2, 3, 4):
                cut(level, at, edge, step)
        low = lowest + 3
        iterate((ya, yb), (xa, xb), low, wide - low)

        def add(i, a, b):
            new_a, new_b = combined(a, b)
            if last:
                x = i - HALO
                total = ua[i, pl.ds(8, nz), :] + damping * new_a + pot[pl.ds(x, nz, stride=rx), :]
                out[pl.ds(x, nz, stride=rx), :] = total
                return
            new_a, new_b = damping * new_a, damping * new_b
            if sweep > 0:
                new_a = new_a + ua[i, pl.ds(8, nz), :]
                new_b = new_b + ub[i, pl.ds(8, nz), :]
            ua[i, pl.ds(8, nz), :] = new_a
            ub[i, pl.ds(8, nz), :] = new_b

        def span(first, end, factor):
            def body(i, carry):
                a, b = read_row(xa, xb, i, nz)
                if factor is not None:
                    a, b = a * factor, b * factor
                add(i, a, b)
                return carry

            lax.fori_loop(first, end, body, 0)

        first, end = low, wide - low
        if sweep == 0:
            for at, edge, step in ends[2:]:
                for j in range(3):
                    i = edge + step * j
                    a, b = read_row(xa, xb, i, nz)
                    c_a, c_b = read_row(cut_a, cut_b, at + 3 + j, nz)
                    add(i, a + c_a, b + c_b)
            first, end = low + 3, wide - low - 3
        span(first, mid_low - 2, 1.0 + has_low)
        span(mid_low + 1, mid_high, None)
        span(mid_high + 3, end, 1.0 + has_high)
        for (at, edge, step), has in zip(ends[:2], (has_low, has_high)):
            for j in range(3):
                i = edge + step * j
                a, b = read_row(xa, xb, i, nz)
                c_a, c_b = read_row(cut_a, cut_b, at + 3 + j, nz)
                add(i, a + has * c_a, b + has * c_b)


def vmem():
    return pl.BlockSpec(memory_space=pltpu.VMEM)


def smem():
    return pl.BlockSpec(memory_space=pltpu.SMEM)


def call(kernel, ins, outs, scratch=()):
    return pl.pallas_call(
        kernel,
        in_specs=ins,
        out_specs=jax.tree.map(lambda _: vmem(), outs),
        out_shape=outs,
        scratch_shapes=list(scratch),
        compiler_params=pltpu.CompilerParams(vmem_limit_bytes=50 << 20),
    )


def shifted(value, axis, steps):
    count = lax.axis_size(axis)
    first, last = max(0, -steps), min(count, count - steps)
    return lax.ppermute(value, axis, [(source, source + steps) for source in range(first, last)])


def on_device(potential, labels, voltages, ion_blocks, owner_map):
    nz, rx, ry = potential.shape
    wide = rx + 2 * HALO
    blocks = ion_blocks[0]
    count, cells = blocks.shape
    tiles = cells // (8 * ry)
    sds = jax.ShapeDtypeStruct
    pot = potential.reshape(nz * rx, ry)
    lab = labels.reshape(nz * rx, ry)
    ny = lax.axis_size("gy")

    slot_rows = 8 * (tiles + (2 if tiles == 1 else 3) + 2)
    slots = call(
        functools.partial(slot_kernel, count, ny, tiles),
        [vmem()],
        sds((count, slot_rows, ry), bf16),
        [pltpu.VMEM((count * tiles * 8, 128), f32)],
    )(blocks)
    got = lax.all_to_all(slots, ("gx", "gy"), split_axis=0, concat_axis=0, tiled=True)

    own_map = jnp.broadcast_to(
        jnp.pad(owner_map[:, 0].astype(f32), (0, 128 - count))[None], (nz, 128)
    )
    strip = sds((2 * HALO + 5, nz, ry), bf16)
    up, down = call(functools.partial(x_pack_kernel, nz, rx), [vmem()] * 3, (strip, strip))(
        pot, lab, own_map
    )
    before = shifted(down, "gx", 1)
    after = shifted(up, "gx", -1)
    field = sds((wide, nz, ry), f32)
    side = sds((wide // 4 + 1, nz, ry), bf16)
    pa, la, left, right = call(
        functools.partial(y_pack_kernel, nz, rx), [vmem()] * 5, (field, field, side, side)
    )(pot, lab, own_map, before, after)
    from_left = shifted(right, "gy", 1)
    from_right = shifted(left, "gy", -1)
    padded = pltpu.VMEM((wide, nz + 16, 128), f32)
    wa, wb, ca, cb, maps = call(
        functools.partial(weight_kernel, nz, rx),
        [smem()] + [vmem()] * 5,
        (field, field, field, field, sds((24, 128), jnp.int32)),
        [padded, padded, pltpu.VMEM((wide, nz, 128), f32)],
    )(voltages, pa, la, from_left, from_right, left)
    cuts = pltpu.VMEM((24, nz + 16, 128), f32)
    plane = pltpu.VMEM(((nz + 1) * (rx + 32), 128), f32)
    out = call(
        functools.partial(sweep_kernel, nz, rx, count, tiles),
        [smem()] + [vmem()] * 6,
        sds((nz * rx, ry), f32),
        [padded] * 8 + [cuts, cuts] + [plane] * 3 + [pltpu.VMEM((wide, nz, 128), f32)] * 2,
    )(maps, got, wa, wb, ca, cb, pot)
    return out.reshape(nz, rx, ry)


def solution(mesh):
    placed = (
        P(None, "gx", "gy"),
        P(None, "gx", "gy"),
        P(),
        P(("gx", "gy"), None, None),
        P(None, ("gx", "gy")),
    )
    return jax.shard_map(
        on_device, mesh=mesh, in_specs=placed, out_specs=P(None, "gx", "gy"), check_vma=False
    )
```

profile of v0, /device:TPU:19, one launch (start us, length us, event | category | flops | bytes accessed | tf_op | source)
XLA Modules:
  0.0 124.6 jit_solution(3967342323246666638)
XLA Ops:
  0.0 0.0 copy-start.5
  0.0 0.9 copy-done.5
  1.0 4.2 %shard_map.58 = bf16[32,72,128]{2,1,0:T(8,128)(2,1)} custom-call(bf16[32,4096]{1,0:T(8,128)(2,1)S(1)} %bitcast.11), custom_call_target="tpu_custom_call" | custom-call | tf_op jit(solution)/shard_map/pallas_call | solution.py:502
  5.1 0.0 copy-start.7
  5.1 0.0 copy-start
  5.1 0.0 copy-start.1
  5.1 6.2 %all-to-all-start = ((bf16[32,72,128]{2,1,0:T(8,128)(2,1)}), bf16[32,72,128]{2,1,0:T(8,128)(2,1)S(1)}, u32[]{:S(2)}, u32[]{:S(2)}) async-start(bf16[32,72,128]{2,1,0:T(8,128)(2,1)} %shard_map.58), calls=%async_computation | async-start | bytes 1179648 | tf_op jit(solution)/shard_map/all_to_all | solution.py:508
  11.3 0.0 copy-done.7
  11.4 0.0 copy-done
  11.4 0.0 copy-done.1
  11.4 0.2 shard_map.55
  11.7 3.1 %collective-permute-start = (bf16[29,16,128]{2,1,0:T(8,128)(2,1)S(1)}, bf16[29,16,128]{2,1,0:T(8,128)(2,1)S(1)}, u32[]{:S(2)}, u32[]{:S(2)}) collective-permute-start(bf16[29,16,128]{2,1,0:T(8,128)(2,1)S(1)} %get-tuple-element.16), channel_id=1, source_target_pairs={{0,8},{8,16},{16,24},{1,9},{9,17},{17,25},{2,10},{10,18},{18,26},{... | collective-permute-start | bytes 356360 | tf_op jit(solution)/shard_map/ppermute | solution.py:487
  14.8 2.2 %collective-permute-start.1 = (bf16[29,16,128]{2,1,0:T(8,128)(2,1)S(1)}, bf16[29,16,128]{2,1,0:T(8,128)(2,1)S(1)}, u32[]{:S(2)}, u32[]{:S(2)}) collective-permute-start(bf16[29,16,128]{2,1,0:T(8,128)(2,1)S(1)} %get-tuple-element.17), channel_id=1, source_target_pairs={{8,0},{16,8},{24,16},{9,1},{17,9},{25,17},{10,2},{18,10},{26,18},{... | collective-permute-start | bytes 356360 | tf_op jit(solution)/shard_map/ppermute | solution.py:487
  17.0 3.2 %collective-permute-done.before = bf16[29,16,128]{2,1,0:T(8,128)(2,1)S(1)} collective-permute-done((bf16[29,16,128]{2,1,0:T(8,128)(2,1)S(1)}, bf16[29,16,128]{2,1,0:T(8,128)(2,1)S(1)}, u32[]{:S(2)}, u32[]{:S(2)}) %collective-permute-start) | collective-permute-done | bytes 118816 | tf_op jit(solution)/shard_map/ppermute | solution.py:487
  20.2 4.6 %collective-permute-done.1.after = bf16[29,16,128]{2,1,0:T(8,128)(2,1)S(1)} collective-permute-done((bf16[29,16,128]{2,1,0:T(8,128)(2,1)S(1)}, bf16[29,16,128]{2,1,0:T(8,128)(2,1)S(1)}, u32[]{:S(2)}, u32[]{:S(2)}) %collective-permute-start.1) | collective-permute-done | bytes 118816 | tf_op jit(solution)/shard_map/ppermute | solution.py:487
  24.7 4.3 %shard_map.56 = (f32[88,16,128]{2,1,0:T(8,128)S(1)}, f32[88,16,128]{2,1,0:T(8,128)S(1)}, bf16[23,16,128]{2,1,0:T(8,128)(2,1)S(1)}, bf16[23,16,128]{2,1,0:T(8,128)(2,1)S(1)}) custom-call(f32[1024,128]{1,0:T(8,128)S(1)} %bitcast.7, s32[1024,128]{1,0:T(8,128)S(1)} %bitcast.10, f32[16,128]{1,0:T(8,128)S(1)} %broadcast_in_dim.2.own_map, ...), custom_call_target="tpu_custom_call" | custom-call | tf_op jit(solution)/shard_map/pallas_call | solution.py:521
  29.0 0.0 copy-start.4
  29.0 0.9 copy-done.4
  29.9 3.2 %collective-permute-start.3 = (bf16[23,16,128]{2,1,0:T(8,128)(2,1)S(1)}, bf16[23,16,128]{2,1,0:T(8,128)(2,1)S(1)}, u32[]{:S(2)}, u32[]{:S(2)}) collective-permute-start(bf16[23,16,128]{2,1,0:T(8,128)(2,1)S(1)} %get-tuple-element.21.own_side), channel_id=1, source_target_pairs={{1,0},{2,1},{3,2},{4,3},{5,4},{6,5},{7,6},{9,8},{10,9},{11,10},{12... | collective-permute-start | bytes 282632 | tf_op jit(solution)/shard_map/ppermute | solution.py:487
  33.1 2.7 %collective-permute-start.2 = (bf16[23,16,128]{2,1,0:T(8,128)(2,1)S(1)}, bf16[23,16,128]{2,1,0:T(8,128)(2,1)S(1)}, u32[]{:S(2)}, u32[]{:S(2)}) collective-permute-start(bf16[23,16,128]{2,1,0:T(8,128)(2,1)S(1)} %get-tuple-element.20), channel_id=1, source_target_pairs={{0,1},{1,2},{2,3},{3,4},{4,5},{5,6},{6,7},{8,9},{9,10},{10,11},{11... | collective-permute-start | bytes 282632 | tf_op jit(solution)/shard_map/ppermute | solution.py:487
  35.8 0.3 collective-permute-done.3.from_right
  36.1 1.3 %collective-permute-done.2.from_left = bf16[23,16,128]{2,1,0:T(8,128)(2,1)S(1)} collective-permute-done((bf16[23,16,128]{2,1,0:T(8,128)(2,1)S(1)}, bf16[23,16,128]{2,1,0:T(8,128)(2,1)S(1)}, u32[]{:S(2)}, u32[]{:S(2)}) %collective-permute-start.2) | collective-permute-done | bytes 94240 | tf_op jit(solution)/shard_map/ppermute | solution.py:487
  37.4 0.0 copy-start.6
  37.4 0.7 copy-done.6
  38.1 16.4 %shard_map.57 = (f32[88,16,128]{2,1,0:T(8,128)S(1)}, f32[88,16,128]{2,1,0:T(8,128)S(1)}, f32[88,16,128]{2,1,0:T(8,128)S(1)}, f32[88,16,128]{2,1,0:T(8,128)S(1)}, s32[24,128]{1,0:T(8,128)S(1)}) custom-call(f32[2]{0:T(128)S(1)} %copy-done.6, f32[88,16,128]{2,1,0:T(8,128)S(1)} %get-tuple-element.18.pa, f32[88,16,128]{2,1,0:T(8,128)} %copy-done.4, ...), custom_call_target="tpu_custom_call" | custom-call | tf_op jit(solution)/shard_map/pallas_call | solution.py:527
  54.5 0.0 copy-start.2
  54.5 0.9 copy-done.2
  55.4 0.0 all-to-all-done.got
  55.4 0.0 copy-start.3
  55.4 1.1 copy-done.3
  56.5 68.1 %shard_map.59 = f32[1024,128]{1,0:T(8,128)} custom-call(s32[24,128]{1,0:T(8,128)S(1)} %get-tuple-element.22.maps, bf16[32,72,128]{2,1,0:T(8,128)(2,1)S(1)} %all-to-all-done.got, f32[88,16,128]{2,1,0:T(8,128)S(1)} %get-tuple-element.23.wa, f32[88,16,128]{2,1,0:T(8,128)S(1)} %get-tuple-element.24.wb, f32[88,16,128]{2,1,0:T(8,128)S(1)} %get-tuple-element.25.ca, ...), custom_call_target="tpu_custom_call" | custom-call | tf_op jit(solution)/shard_map/pallas_call | solution.py:535
  (3 shorter events, 0.0 us)
Async XLA Ops:
  0.0 0.9 copy-start.5
  5.1 6.2 %copy-start.7 = (s32[32,1]{0,1:T(1,128)S(1)}, s32[32,1]{0,1:T(1,128)}, u32[]{:S(2)}) copy-start(s32[32,1]{0,1:T(1,128)} %param.9) | copy-start | bytes 388
  5.1 6.3 %copy-start = (f32[16,64,128]{2,1,0:T(8,128)S(1)}, f32[16,64,128]{2,1,0:T(8,128)}, u32[]{:S(2)}) copy-start(f32[16,64,128]{2,1,0:T(8,128)} %param.5) | copy-start | bytes 1572868
  5.1 6.3 %copy-start.1 = (s32[16,64,128]{2,1,0:T(8,128)S(1)}, s32[16,64,128]{2,1,0:T(8,128)}, u32[]{:S(2)}) copy-start(s32[16,64,128]{2,1,0:T(8,128)} %param.6) | copy-start | bytes 1572868
  5.1 50.3 %all-to-all-start = ((bf16[32,72,128]{2,1,0:T(8,128)(2,1)}), bf16[32,72,128]{2,1,0:T(8,128)(2,1)S(1)}, u32[]{:S(2)}, u32[]{:S(2)}) async-start(bf16[32,72,128]{2,1,0:T(8,128)(2,1)} %shard_map.58), calls=%async_computation | async-start | bytes 1179648 | tf_op jit(solution)/shard_map/all_to_all | solution.py:508
  11.7 8.5 %collective-permute-start = (bf16[29,16,128]{2,1,0:T(8,128)(2,1)S(1)}, bf16[29,16,128]{2,1,0:T(8,128)(2,1)S(1)}, u32[]{:S(2)}, u32[]{:S(2)}) collective-permute-start(bf16[29,16,128]{2,1,0:T(8,128)(2,1)S(1)} %get-tuple-element.16), channel_id=1, source_target_pairs={{0,8},{8,16},{16,24},{1,9},{9,17},{17,25},{2,10},{10,18},{18,26},{... | collective-permute-start | bytes 356360 | tf_op jit(solution)/shard_map/ppermute | solution.py:487
  14.8 10.0 %collective-permute-start.1 = (bf16[29,16,128]{2,1,0:T(8,128)(2,1)S(1)}, bf16[29,16,128]{2,1,0:T(8,128)(2,1)S(1)}, u32[]{:S(2)}, u32[]{:S(2)}) collective-permute-start(bf16[29,16,128]{2,1,0:T(8,128)(2,1)S(1)} %get-tuple-element.17), channel_id=1, source_target_pairs={{8,0},{16,8},{24,16},{9,1},{17,9},{25,17},{10,2},{18,10},{26,18},{... | collective-permute-start | bytes 356360 | tf_op jit(solution)/shard_map/ppermute | solution.py:487
  29.0 0.9 copy-start.4
  29.9 6.3 %collective-permute-start.3 = (bf16[23,16,128]{2,1,0:T(8,128)(2,1)S(1)}, bf16[23,16,128]{2,1,0:T(8,128)(2,1)S(1)}, u32[]{:S(2)}, u32[]{:S(2)}) collective-permute-start(bf16[23,16,128]{2,1,0:T(8,128)(2,1)S(1)} %get-tuple-element.21.own_side), channel_id=1, source_target_pairs={{1,0},{2,1},{3,2},{4,3},{5,4},{6,5},{7,6},{9,8},{10,9},{11,10},{12... | collective-permute-start | bytes 282632 | tf_op jit(solution)/shard_map/ppermute | solution.py:487
  33.1 4.3 %collective-permute-start.2 = (bf16[23,16,128]{2,1,0:T(8,128)(2,1)S(1)}, bf16[23,16,128]{2,1,0:T(8,128)(2,1)S(1)}, u32[]{:S(2)}, u32[]{:S(2)}) collective-permute-start(bf16[23,16,128]{2,1,0:T(8,128)(2,1)S(1)} %get-tuple-element.20), channel_id=1, source_target_pairs={{0,1},{1,2},{2,3},{3,4},{4,5},{5,6},{6,7},{8,9},{9,10},{10,11},{11... | collective-permute-start | bytes 282632 | tf_op jit(solution)/shard_map/ppermute | solution.py:487
  37.4 0.7 copy-start.6
  54.5 0.9 copy-start.2
  55.4 1.1 copy-start.3
where the time goes:
time: 126 us; the launch traced here: 125 us
  Pallas kernels  93.2 us (74%)
  starting transfers between devices  17.4 us (14%)
  waiting for transfers between devices  9.37 us (7%)
  local copies, waits for them, and re-layouts  4.45 us (4%)
    pallas_call x1, Pallas kernels, on_device(): call(functools.partial(sweep_kernel, nz, rx, count, tiles), [smem()] + [v...  68.1 us
    pallas_call x1, Pallas kernels, on_device(): call(functools.partial(weight_kernel, nz, rx), [smem()] + [vmem()] * 5, (...  16.4 us
    ppermute x4, starting transfers between devices, shifted(): lax.ppermute(value, axis, [(source, source + steps) for source in range(f...  11.2 us
    ppermute x4, waiting for transfers between devices, shifted(): lax.ppermute(value, axis, [(source, source + steps) for source in range(f...  9.36 us
    all_to_all x1, starting transfers between devices, on_device(): lax.all_to_all(slots, ('gx', 'gy'), split_axis=0, concat_axis=0, tiled=True)  6.22 us
    unnamed x16, local copies, waits for them, and re-layouts  4.45 us
    pallas_call x1, Pallas kernels, on_device(): call(functools.partial(y_pack_kernel, nz, rx), [vmem()] * 5, (field, fiel...  4.26 us
    pallas_call x1, Pallas kernels, on_device(): call(functools.partial(slot_kernel, count, ny, tiles), [vmem()], sds((cou...  4.16 us
  transfers between devices with their start and end apart: 5, of which 4 were waited for; matrix products, arithmetic and copies ran while one was open for 0% of the time, Pallas kernels for 17%

commit v1 on v0

v1 whole, which is shorter than its diff:
```python
import functools

import jax
import jax.numpy as jnp
from jax import lax
from jax.experimental import pallas as pl
from jax.experimental.pallas import tpu as pltpu
from jax.sharding import PartitionSpec as P

HALO = 12
debye_term = 1.0
damping = 0.5

f32 = jnp.float32
bf16 = jnp.bfloat16


def lane_iota(rows):
    return lax.broadcasted_iota(jnp.int32, (rows, 128), 1)


def between(lane, low, high):
    return (lane >= low) & (lane < high)


def roll(value, shift):
    shift = shift % 128
    return value if shift == 0 else pltpu.roll(value, shift, 1)


def x_pack_kernel(nz, rx, pot, lab, own_map, up, down):
    def row(ref, x):
        return ref[pl.ds(x, nz, stride=rx), :]

    for out, first, near in ((up, 0, 0), (down, rx - HALO, rx - 4)):
        for i in range(HALO):
            value = row(pot, first + i)
            high = value.astype(bf16)
            out[i] = high
            offset = first + i - near
            if 0 <= offset < 4:
                out[HALO + offset] = (value - high.astype(f32)).astype(bf16)
            out[HALO + 4 + i] = (row(lab, first + i) + 1).astype(f32).astype(bf16)
        out[2 * HALO + 4] = own_map[...].astype(bf16)


def y_pack_kernel(nz, rx, pot, lab, own_map, before, after, pa, la, left, right):
    wide = rx + 2 * HALO
    for i in range(HALO):
        value = before[i].astype(f32)
        if i >= HALO - 4:
            value = value + before[HALO + i - (HALO - 4)].astype(f32)
        pa[i] = value
        la[i] = before[HALO + 4 + i].astype(f32)
        value = after[i].astype(f32)
        if i < 4:
            value = value + after[HALO + i].astype(f32)
        pa[HALO + rx + i] = value
        la[HALO + rx + i] = after[HALO + 4 + i].astype(f32)

    def copy_rows(step, carry):
        for q in range(4):
            x = step * 4 + q
            pa[HALO + x] = pot[pl.ds(x, nz, stride=rx), :]
            la[HALO + x] = (lab[pl.ds(x, nz, stride=rx), :] + 1).astype(f32)
        return carry

    lax.fori_loop(0, rx // 4, copy_rows, 0)

    lane = lane_iota(nz)
    is_low = between(lane, 12, 16)
    is_label = lane >= 16
    group_of = lane // 32

    def group(g):
        to_left = jnp.zeros((nz, 128), f32)
        to_right = jnp.zeros((nz, 128), f32)
        for q in range(4):
            value = pa[g * 4 + q]
            code = la[g * 4 + q]
            high = value.astype(bf16).astype(f32)
            low = value - high
            one = jnp.where(is_label, roll(code, 16), jnp.where(is_low, roll(low, 12), high))
            two = jnp.where(is_label, roll(code, 28), jnp.where(is_low, roll(low, 16), roll(high, 12)))
            here = group_of == q
            to_left = jnp.where(here, roll(one, 32 * q), to_left)
            to_right = jnp.where(here, roll(two, 32 * q), to_right)
        left[g] = to_left.astype(bf16)
        right[g] = to_right.astype(bf16)

    def groups(first, size):
        for k in range(size):
            group(first + k)

    chunked(0, wide // 4, 4, groups)
    row = lax.broadcasted_iota(jnp.int32, (nz, 128), 0)
    maps = jnp.where(
        row == 0,
        before[2 * HALO + 4].astype(f32),
        jnp.where(row == 1, own_map[...], after[2 * HALO + 4].astype(f32)),
    ).astype(bf16)
    left[wide // 4] = maps
    right[wide // 4] = maps


NOWHERE = -1000


def place_of(column):
    return jnp.where(column < 128, 2 * column, 2 * column - 255)


def cell_of(place):
    cell = jnp.where(place <= 136, place, NOWHERE)
    cell = jnp.where(between(place, 148, 169), place - 160, cell)
    cell = jnp.where(between(place, 183, 204), place - 64, cell)
    return jnp.where(place >= 247, place - 256, cell)


def grid_of(rows, columns):
    return (
        lax.broadcasted_iota(jnp.int32, (rows, columns), 0),
        lax.broadcasted_iota(jnp.int32, (rows, columns), 1),
    )


def ones_where(condition):
    return jnp.where(condition, 1.0, 0.0).astype(bf16)


def parts_of(value):
    high = value.astype(bf16)
    rest = value - high.astype(f32)
    middle = rest.astype(bf16)
    return high, middle, (rest - middle.astype(f32)).astype(bf16)


def product(left, right):
    return jnp.dot(left, right, preferred_element_type=f32)


def read(ref, i, nz):
    return ref[i, pl.ds(8, nz), :]


def neighbour_rows(refs, i, nz, low_row, high_row):
    even, odd = read(refs[0], i, nz), read(refs[1], i, nz)
    out = [odd + roll(odd, 1), even + roll(even, 127)]
    for t in (0, 1):
        out[t] = out[t] + (refs[t][i, pl.ds(7, nz), :] + refs[t][i, pl.ds(9, nz), :])
        for beside in (low_row, high_row):
            if beside is not None:
                out[t] = out[t] + beside[t]
    return out


def read_row(refs, i, nz):
    return read(refs[0], i, nz), read(refs[1], i, nz)


def clear_pads(refs, count, nz):
    zero = jnp.zeros((count, 8, 128), f32)
    for ref in refs:
        ref[:, pl.ds(0, 8), :] = zero
        ref[:, pl.ds(8 + nz, 8), :] = zero


def chunked(low, high, most, fn):
    count = -(-(high - low) // most)
    size = -(-(high - low) // count)
    if count == 1:
        fn(low, size)
        return

    def body(step, carry):
        fn(jnp.minimum(low + step * size, high - size), size)
        return carry

    lax.fori_loop(0, count, body, 0)


def absent(place):
    index = lax.axis_index("gy")
    none_before = between(place, 148, 169) & (index == 0)
    none_after = between(place, 183, 204) & (index == lax.axis_size("gy") - 1)
    return none_before | none_after


def weight_kernel(nz, rx, volts, pa, la, from_left, from_right, own_side, we, wo, ce, co, maps, ppe, ppo, lbe, lbo):
    wide = rx + 2 * HALO
    groups = wide // 4
    clear_pads((ppe, ppo), wide, nz)
    row, column = grid_of(128, 256)
    cell = cell_of(place_of(column))
    own = ones_where(row == cell)
    row, column = grid_of(32, 256)
    cell = cell_of(place_of(column))
    low_side = cell < 0
    from_low, from_high = cell + HALO, cell - 128
    pot_low = ones_where(
        low_side & (((row < HALO) & (row == from_low)) | (between(row, 12, 16) & (row == from_low + 4)))
    )
    pot_high = ones_where(
        (cell >= 128) & (((row < HALO) & (row == from_high)) | (between(row, 12, 16) & (row == from_high + 12)))
    )
    lab_low = ones_where(low_side & between(row, 16, 28) & (row == from_low + 16))
    lab_high = ones_where((cell >= 128) & between(row, 16, 28) & (row == from_high + 16))

    def moved(matrix, q):
        pieces = [jnp.zeros((32, 256), bf16)] * 4
        pieces[q] = matrix
        return jnp.concatenate(pieces, axis=0)

    flat = (groups * nz, 128)
    left = from_left[pl.ds(0, groups)].reshape(flat)
    right = from_right[pl.ds(0, groups)].reshape(flat)
    for q in range(4):
        value = pa[pl.ds(q, groups, stride=4)].reshape(flat)
        high, middle, low = parts_of(value)
        pot = product(jnp.concatenate([high, left], axis=1), jnp.concatenate([own, moved(pot_low, q)], axis=0))
        pot = pot + product(
            jnp.concatenate([middle, right], axis=1), jnp.concatenate([own, moved(pot_high, q)], axis=0)
        )
        pot = (pot + product(low, own)).reshape(groups, nz, 256)
        ppe[pl.ds(q, groups, stride=4), pl.ds(8, nz), :] = pot[:, :, :128]
        ppo[pl.ds(q, groups, stride=4), pl.ds(8, nz), :] = pot[:, :, 128:]
        code = la[pl.ds(q, groups, stride=4)].reshape(flat).astype(bf16)
        lab = product(jnp.concatenate([code, left], axis=1), jnp.concatenate([own, moved(lab_low, q)], axis=0))
        lab = (lab + product(right, moved(lab_high, q))).reshape(groups, nz, 256)
        lbe[pl.ds(q, groups, stride=4)] = lab[:, :, :128]
        lbo[pl.ds(q, groups, stride=4)] = lab[:, :, 128:]
    lane = lane_iota(nz)
    kept = []
    for t in (0, 1):
        place = 2 * lane + t
        keep = (place < 136) | between(place, 149, 168) | between(place, 184, 203) | (place >= 248)
        kept.append(keep & ~absent(place))
    v0 = volts[0]
    v1 = volts[1]

    def rows(first, size):
        for k in range(size):
            i = first + k
            near = neighbour_rows((ppe, ppo), i, nz, read_row((ppe, ppo), i - 1, nz), read_row((ppe, ppo), i + 1, nz))
            for t, (p_ref, code_ref, w_out, c_out) in enumerate(((ppe, lbe, we, ce), (ppo, lbo, wo, co))):
                p = read(p_ref, i, nz)
                code = jnp.where(kept[t], code_ref[i], 0.0)
                growth = jnp.exp(p)
                inverse = 1.0 / (6.0 + debye_term * growth)
                plasma = between(code, 0.5, 1.5)
                edge = jnp.where(code < 2.5, v0, v1)
                w = jnp.where(plasma, (near[t] - 6.0 * p - debye_term * growth) * inverse, edge - p)
                w_out[i] = jnp.where(code > 0.5, w, 0.0)
                c_out[i] = jnp.where(plasma, inverse, 0.0)

    chunked(1, wide - 1, 22, rows)
    zero = jnp.zeros((nz, 128), f32)
    for i in (0, wide - 1):
        for ref in (we, wo, ce, co):
            ref[i] = zero
    for at, ref in ((0, from_left), (8, own_side), (16, from_right)):
        maps[pl.ds(at, 8), :] = ref[groups].astype(f32)[0:8].astype(jnp.int32)


def slot_kernel(count, ny, tiles, blocks, out, field):
    rows = tiles * 8
    for r in range(rows):
        field[pl.ds(r, count, stride=rows), :] = blocks[:, pl.ds(r * 128, 128)].astype(f32)
    lane = lane_iota(8)
    sub = lax.broadcasted_iota(jnp.int32, (8, 128), 0)

    def one(k, carry):
        def tile(offset, t):
            brick = lax.rem(k + offset + count, count)
            return field[pl.ds(pl.multiple_of(brick * rows + t * 8, 8), 8), :]

        parts = [tile(0, t) for t in range(tiles)]
        if tiles == 1:
            parts += [tile(ny, 0), tile(-ny, 0)]
        else:
            mixed = jnp.where(sub < 4, tile(ny, 1), tile(-ny, tiles - 2))
            parts += [tile(ny, 0), mixed, tile(-ny, tiles - 1)]

        def pair(offset, t, at):
            low = roll(tile(offset - 1, t), 12 + at)
            high = roll(tile(offset + 1, t), 16 + at)
            return jnp.where(between(lane, at, at + 12), low, high)

        sides = jnp.zeros((8, 128), f32)
        for t in range(tiles):
            sides = jnp.where(between(lane, 32 * t, 32 * t + 32), pair(0, t, 32 * t), sides)
        corners = jnp.where(lane < 32, pair(ny, 0, 0), pair(-ny, tiles - 1, 32))
        if tiles > 1:
            second = jnp.where(lane < 96, pair(ny, 1, 64), pair(-ny, tiles - 2, 96))
            corners = jnp.where(lane < 64, corners, second)
        parts += [sides, corners]
        out[k] = jnp.concatenate(parts, axis=0).astype(bf16)
        return carry

    def some(step, carry):
        for k in range(4):
            one(step * 4 + k, carry)
        return carry

    lax.fori_loop(0, count // 4, some, 0)


def sweep_kernel(nz, rx, count, tiles, maps, got, we, wo, ce, co, pot, out, *scratch):
    (re, ro, xe, xo, ye, yo, ue, uo, cut_e, cut_o, ch_a, ch_l, ch_r, ve, vo) = scratch
    rhs, xs, ys, us, cuts = (re, ro), (xe, xo), (ye, yo), (ue, uo), (cut_e, cut_o)
    weights, charged, couplings = (we, wo), (ve, vo), (ce, co)
    wide = rx + 2 * HALO
    tall = rx + 32
    per_plane = rx // (8 * tiles)
    lane = lane_iota(nz)
    index_x, index_y = lax.axis_index("gx"), lax.axis_index("gy")
    low_x, high_x = index_x > 0, index_x < lax.axis_size("gx") - 1
    has_low, has_high = jnp.where(low_x, 1.0, 0.0), jnp.where(high_x, 1.0, 0.0)
    clear_pads(rhs + xs + ys + us, wide, nz)
    clear_pads(cuts, cut_e.shape[0], nz)

    def place(p):
        slot = got[p].astype(f32)
        pieces = [slot[8 * t : 8 * t + 8] for t in range(slot.shape[0] // 8)]

        def where_to(which, side):
            index = maps[which, p]
            z = index // per_plane
            part = index - z * per_plane
            if side == 0:
                return z, part, None
            depth = part if side > 0 else per_plane - 1 - part
            ok = depth * 8 * tiles < HALO
            return jnp.where(ok, z, nz), part, jnp.where(ok, depth, 0)

        def put(ref, z, row, value):
            ref[pl.ds(pl.multiple_of(z * tall + row, 8), 8), :] = value

        z, part, _ = where_to(9, 0)
        for t in range(tiles):
            put(ch_a, z, 16 + (part * tiles + t) * 8, pieces[t])
        zp, _, dp = where_to(10, 1)
        zm, _, dm = where_to(8, -1)
        if tiles == 1:
            put(ch_a, zp, 16 + rx + dp * 8, pieces[1])
            put(ch_a, zm, 8 - dm * 8, pieces[2])
            next_piece = 3
        else:
            put(ch_a, zp, 16 + rx, pieces[tiles])
            put(ch_a, zp, 24 + rx, pieces[tiles + 1])
            put(ch_a, zm, 0, pieces[tiles + 1])
            put(ch_a, zm, 8, pieces[tiles + 2])
            next_piece = tiles + 3
        sides = pieces[next_piece]
        corners = pieces[next_piece + 1]
        zl, part_l, _ = where_to(1, 0)
        zr, part_r, _ = where_to(17, 0)
        for t in range(tiles):
            value = roll(sides, -32 * t)
            put(ch_l, zl, 16 + (part_l * tiles + t) * 8, value)
            put(ch_r, zr, 16 + (part_r * tiles + t) * 8, value)
        for at, side in ((0, 1), (32, -1)):
            value = roll(corners, -at)
            second = None if tiles == 1 else roll(corners, -at - 64)
            for which, ref in ((1 + side, ch_l), (17 + side, ch_r)):
                z, _, depth = where_to(which, side)
                if tiles == 1:
                    put(ref, z, (16 + rx + depth * 8) if side > 0 else (8 - depth * 8), value)
                else:
                    put(ref, z, (16 + rx) if side > 0 else 8, value)
                    put(ref, z, (24 + rx) if side > 0 else 0, second)

    def place_some(step, carry):
        for k in range(8):
            place(step * 8 + k)
        return carry

    lax.fori_loop(0, count // 8, place_some, 0)

    row, column = grid_of(256, 256)
    cell = cell_of(place_of(column))
    spread = ones_where(
        ((row < 128) & (row == cell))
        | (between(row, 128, 128 + HALO) & (row - (128 + HALO) == cell))
        | (between(row, 144, 144 + HALO) & (row - 16 == cell))
    )
    source = cell_of(place_of(row))
    gather = jnp.where((source == cell) & (cell != NOWHERE), damping, 0.0).astype(bf16)
    row, column = grid_of(256, 128)
    final = ones_where(cell_of(place_of(row)) == column)
    is_low = (lane < HALO) & (index_y > 0)
    is_high = between(lane, 16, 16 + HALO) & (index_y < lax.axis_size("gy") - 1)

    def add_charge(present):
        def rows(first, size):
            both = []
            for k in range(size):
                x = first + k + 4
                a = ch_a[pl.ds(x, nz, stride=tall), :]
                low = ch_l[pl.ds(x, nz, stride=tall), :]
                high = ch_r[pl.ds(x, nz, stride=tall), :]
                strip = jnp.where(is_low, low, jnp.where(is_high, high, 0.0))
                if present is not None:
                    a = jnp.where(present, a, 0.0)
                    strip = jnp.where(present, strip, 0.0)
                both.append(jnp.concatenate([a, strip], axis=1).astype(bf16))
            charge = product(jnp.concatenate(both, axis=0), spread)
            for k in range(size):
                i = first + k
                for t in (0, 1):
                    part = charge[k * nz : (k + 1) * nz, 128 * t : 128 * t + 128]
                    value = weights[t][i] + debye_term * couplings[t][i] * part
                    charged[t][i] = value
                    rhs[t][i, pl.ds(8, nz), :] = value

        return rows

    chunked(1, HALO, HALO, add_charge(low_x))
    chunked(HALO, HALO + rx, 16, add_charge(None))
    chunked(HALO + rx, wide - 1, HALO, add_charge(high_x))

    def iterate(src, dst, low, high):
        def rows(first, size):
            for k in range(size):
                i = first + k
                near = neighbour_rows(src, i, nz, read_row(src, i - 1, nz), read_row(src, i + 1, nz))
                for t in (0, 1):
                    dst[t][i, pl.ds(8, nz), :] = read(rhs[t], i, nz) + couplings[t][i] * near[t]

        chunked(low, high, 28, rows)

    def cut(level, at, edge, step):
        starts = {2: 0, 3: 1, 4: 3}
        whole = {2: rhs, 3: xs, 4: ys}[level]
        for j in range(level - 1):
            i = edge + step * j
            before = at + starts.get(level - 1, 0)
            changed = j < level - 2
            outer = None if j == 0 else read_row(cuts, before + j - 1, nz)
            inner = read_row(cuts, before + j + 1, nz) if j + 1 < level - 2 else read_row(whole, i + step, nz)
            near = neighbour_rows(cuts if changed else whole, before + j if changed else i, nz, outer, inner)
            for t in (0, 1):
                cuts[t][at + starts[level] + j, pl.ds(8, nz), :] = read(rhs[t], i, nz) + couplings[t][i] * near[t]

    ends = [(0, HALO + 7, -1), (6, HALO + rx - 8, 1), (12, HALO - 8, 1), (18, HALO + rx + 7, -1)]
    ghosts = [(2 * lane + t == 168) | (2 * lane + t == 183) | absent(2 * lane + t) for t in (0, 1)]
    own = lane < 64
    for sweep in range(3):
        last = sweep == 2
        lowest = 1 + 4 * sweep
        if sweep > 0:

            def residual(first, size):
                for k in range(size):
                    i = first + k
                    near = neighbour_rows(us, i, nz, read_row(us, i - 1, nz), read_row(us, i + 1, nz))
                    for t in (0, 1):
                        held = jnp.where(ghosts[t], 0.0, charged[t][i] - read(us[t], i, nz))
                        shared = jnp.where(ghosts[t], 0.0, near[t])
                        rhs[t][i, pl.ds(8, nz), :] = held + couplings[t][i] * shared

            chunked(lowest, wide - lowest, 28, residual)
        iterate(rhs, xs, lowest + 1, wide - lowest - 1)
        iterate(xs, ys, lowest + 2, wide - lowest - 2)
        some = ends if sweep == 0 else ends[:2]
        for level in (2, 3, 4):
            for at, edge, step in some:
                cut(level, at, edge, step)
        low, high = lowest + 3, wide - lowest - 3
        iterate(ys, xs, low, high)

        def scale(first, end, factor):
            for i in range(first, end):
                for t in (0, 1):
                    xs[t][i, pl.ds(8, nz), :] = read(xs[t], i, nz) * factor

        def add_cut(at, edge, step, factor, kept):
            for j in range(3):
                i = edge + step * j
                for t in (0, 1):
                    whole = read(xs[t], i, nz)
                    part = read(cuts[t], at + 3 + j, nz)
                    xs[t][i, pl.ds(8, nz), :] = (part + factor * whole) if kept else (whole + factor * part)

        mid_low, mid_high = HALO + 7, HALO + rx - 8
        if sweep == 0:
            add_cut(*ends[2], has_low, True)
            add_cut(*ends[3], has_high, True)
            scale(low + 3, mid_low - 2, 1.0 + has_low)
            scale(mid_high + 3, high - 3, 1.0 + has_high)
        else:
            scale(low, mid_low - 2, 1.0 + has_low)
            scale(mid_high + 3, high, 1.0 + has_high)
        add_cut(*ends[0], has_low, False)
        add_cut(*ends[1], has_high, False)

        def join(first, size):
            flat = (size * nz, 128)
            both = [xs[t][pl.ds(first, size), pl.ds(8, nz), :].reshape(flat) for t in (0, 1)]
            if last:
                keep = lane_iota(size * nz) < 64
                both = [
                    damping * both[t]
                    + jnp.where(keep, us[t][pl.ds(first, size), pl.ds(8, nz), :].reshape(flat), 0.0)
                    for t in (0, 1)
                ]
            parts = parts_of(jnp.concatenate(both, axis=1))
            matrix = final if last else gather
            total = product(parts[2], matrix) + product(parts[1], matrix) + product(parts[0], matrix)
            if last:
                for k in range(size):
                    x = first + k - HALO
                    out[pl.ds(x, nz, stride=rx), :] = total[k * nz : (k + 1) * nz] + pot[pl.ds(x, nz, stride=rx), :]
                return
            for t in (0, 1):
                value = total[:, 128 * t : 128 * t + 128].reshape(size, nz, 128)
                if sweep > 0:
                    value = value + us[t][pl.ds(first, size), pl.ds(8, nz), :]
                us[t][pl.ds(first, size), pl.ds(8, nz), :] = value

        for first in range(low, high, 16):
            join(first, min(16, high - first))


def vmem():
    return pl.BlockSpec(memory_space=pltpu.VMEM)


def smem():
    return pl.BlockSpec(memory_space=pltpu.SMEM)


def call(kernel, ins, outs, scratch=()):
    return pl.pallas_call(
        kernel,
        in_specs=ins,
        out_specs=jax.tree.map(lambda _: vmem(), outs),
        out_shape=outs,
        scratch_shapes=list(scratch),
        compiler_params=pltpu.CompilerParams(vmem_limit_bytes=50 << 20),
    )


def shifted(value, axis, steps):
    count = lax.axis_size(axis)
    first, last = max(0, -steps), min(count, count - steps)
    return lax.ppermute(value, axis, [(source, source + steps) for source in range(first, last)])


def on_device(potential, labels, voltages, ion_blocks, owner_map):
    nz, rx, ry = potential.shape
    wide = rx + 2 * HALO
    blocks = ion_blocks[0]
    count, cells = blocks.shape
    tiles = cells // (8 * ry)
    sds = jax.ShapeDtypeStruct
    pot = potential.reshape(nz * rx, ry)
    lab = labels.reshape(nz * rx, ry)
    ny = lax.axis_size("gy")

    slot_rows = 8 * (tiles + (2 if tiles == 1 else 3) + 2)
    slots = call(
        functools.partial(slot_kernel, count, ny, tiles),
        [vmem()],
        sds((count, slot_rows, ry), bf16),
        [pltpu.VMEM((count * tiles * 8, 128), f32)],
    )(blocks)
    got = lax.all_to_all(slots, ("gx", "gy"), split_axis=0, concat_axis=0, tiled=True)

    own_map = jnp.broadcast_to(
        jnp.pad(owner_map[:, 0].astype(f32), (0, 128 - count))[None], (nz, 128)
    )
    strip = sds((2 * HALO + 5, nz, ry), bf16)
    up, down = call(functools.partial(x_pack_kernel, nz, rx), [vmem()] * 3, (strip, strip))(
        pot, lab, own_map
    )
    before = shifted(down, "gx", 1)
    after = shifted(up, "gx", -1)
    field = sds((wide, nz, ry), f32)
    side = sds((wide // 4 + 1, nz, ry), bf16)
    pa, la, left, right = call(
        functools.partial(y_pack_kernel, nz, rx), [vmem()] * 5, (field, field, side, side)
    )(pot, lab, own_map, before, after)
    from_left = shifted(right, "gy", 1)
    from_right = shifted(left, "gy", -1)
    padded = pltpu.VMEM((wide, nz + 16, 128), f32)
    we, wo, ce, co, maps = call(
        functools.partial(weight_kernel, nz, rx),
        [smem()] + [vmem()] * 5,
        (field, field, field, field, sds((24, 128), jnp.int32)),
        [padded, padded] + [pltpu.VMEM((wide, nz, 128), f32)] * 2,
    )(voltages, pa, la, from_left, from_right, left)
    cuts = pltpu.VMEM((24, nz + 16, 128), f32)
    plane = pltpu.VMEM(((nz + 1) * (rx + 32), 128), f32)
    out = call(
        functools.partial(sweep_kernel, nz, rx, count, tiles),
        [smem()] + [vmem()] * 6,
        sds((nz * rx, ry), f32),
        [padded] * 8 + [cuts, cuts] + [plane] * 3 + [pltpu.VMEM((wide, nz, 128), f32)] * 2,
    )(maps, got, we, wo, ce, co, pot)
    return out.reshape(nz, rx, ry)


def solution(mesh):
    placed = (
        P(None, "gx", "gy"),
        P(None, "gx", "gy"),
        P(),
        P(("gx", "gy"), None, None),
        P(None, ("gx", "gy")),
    )
    return jax.shard_map(
        on_device, mesh=mesh, in_specs=placed, out_specs=P(None, "gx", "gy"), check_vma=False
    )
```

time: 126 us -> 58.6 us (0.47)
  the two profiles are of different devices: /device:TPU:19 before, /device:TPU:1 now
where the time goes in v1:
time: 58.6 us; the launch traced here: 58.3 us
  Pallas kernels  25.9 us (44%)
  starting transfers between devices  18.4 us (31%)
  waiting for transfers between devices  9.32 us (16%)
  local copies, waits for them, and re-layouts  4.45 us (8%)
    pallas_call x1, Pallas kernels, on_device(): call(functools.partial(sweep_kernel, nz, rx, count, tiles), [smem()] + [v...  17.3 us
    ppermute x4, starting transfers between devices, shifted(): lax.ppermute(value, axis, [(source, source + steps) for source in range(f...  11.3 us
    ppermute x4, waiting for transfers between devices, shifted(): lax.ppermute(value, axis, [(source, source + steps) for source in range(f...  9.32 us
    all_to_all x1, starting transfers between devices, on_device(): lax.all_to_all(slots, ('gx', 'gy'), split_axis=0, concat_axis=0, tiled=True)  7.1 us
    unnamed x16, local copies, waits for them, and re-layouts  4.44 us
    pallas_call x1, Pallas kernels, on_device(): call(functools.partial(weight_kernel, nz, rx), [smem()] + [vmem()] * 5, (...  3.65 us
    pallas_call x1, Pallas kernels, on_device(): call(functools.partial(y_pack_kernel, nz, rx), [vmem()] * 5, (field, fiel...  2.45 us
    pallas_call x1, Pallas kernels, on_device(): call(functools.partial(slot_kernel, count, ny, tiles), [vmem()], sds((cou...  2.3 us
  transfers between devices with their start and end apart: 5, of which 4 were waited for; matrix products, arithmetic and copies ran while one was open for 0% of the time, Pallas kernels for 11%

profile of v1, /device:TPU:1, one launch (start us, length us, event | category | flops | bytes accessed | tf_op | source)
XLA Modules:
  0.0 58.3 jit_solution(12430666240271680699)
XLA Ops:
  0.0 0.0 copy-start.5
  0.0 0.9 %copy-done.5 = bf16[1,32,4096]{2,1,0:T(8,128)(2,1)S(1)} copy-done((bf16[1,32,4096]{2,1,0:T(8,128)(2,1)S(1)}, bf16[1,32,4096]{2,1,0:T(8,128)(2,1)}, u32[]{:S(2)}) %copy-start.5) | copy-done | bytes 262168
  1.0 2.3 %shard_map.58 = bf16[32,72,128]{2,1,0:T(8,128)(2,1)} custom-call(bf16[32,4096]{1,0:T(8,128)(2,1)S(1)} %bitcast.11), custom_call_target="tpu_custom_call" | custom-call | tf_op jit(solution)/shard_map/pallas_call | solution.py:562
  3.3 0.0 copy-start.7
  3.3 0.0 copy-start
  3.3 0.0 copy-start.1
  3.3 7.1 %all-to-all-start = ((bf16[32,72,128]{2,1,0:T(8,128)(2,1)}), bf16[32,72,128]{2,1,0:T(8,128)(2,1)S(1)}, u32[]{:S(2)}, u32[]{:S(2)}) async-start(bf16[32,72,128]{2,1,0:T(8,128)(2,1)} %shard_map.58), calls=%async_computation | async-start | bytes 1179648 | tf_op jit(solution)/shard_map/all_to_all | solution.py:568
  10.4 0.0 copy-done.7
  10.4 0.0 copy-done
  10.4 0.0 copy-done.1
  10.4 0.2 shard_map.55
  10.7 3.3 %collective-permute-start = (bf16[29,16,128]{2,1,0:T(8,128)(2,1)S(1)}, bf16[29,16,128]{2,1,0:T(8,128)(2,1)S(1)}, u32[]{:S(2)}, u32[]{:S(2)}) collective-permute-start(bf16[29,16,128]{2,1,0:T(8,128)(2,1)S(1)} %get-tuple-element.16), channel_id=1, source_target_pairs={{0,8},{8,16},{16,24},{1,9},{9,17},{17,25},{2,10},{10,18},{18,26},{... | collective-permute-start | bytes 356360 | tf_op jit(solution)/shard_map/ppermute | solution.py:547
  14.0 1.3 %collective-permute-start.1 = (bf16[29,16,128]{2,1,0:T(8,128)(2,1)S(1)}, bf16[29,16,128]{2,1,0:T(8,128)(2,1)S(1)}, u32[]{:S(2)}, u32[]{:S(2)}) collective-permute-start(bf16[29,16,128]{2,1,0:T(8,128)(2,1)S(1)} %get-tuple-element.17), channel_id=1, source_target_pairs={{8,0},{16,8},{24,16},{9,1},{17,9},{25,17},{10,2},{18,10},{26,18},{... | collective-permute-start | bytes 356360 | tf_op jit(solution)/shard_map/ppermute | solution.py:547
  15.3 2.3 %collective-permute-done.before = bf16[29,16,128]{2,1,0:T(8,128)(2,1)S(1)} collective-permute-done((bf16[29,16,128]{2,1,0:T(8,128)(2,1)S(1)}, bf16[29,16,128]{2,1,0:T(8,128)(2,1)S(1)}, u32[]{:S(2)}, u32[]{:S(2)}) %collective-permute-start) | collective-permute-done | bytes 118816 | tf_op jit(solution)/shard_map/ppermute | solution.py:547
  17.5 5.5 %collective-permute-done.1.after = bf16[29,16,128]{2,1,0:T(8,128)(2,1)S(1)} collective-permute-done((bf16[29,16,128]{2,1,0:T(8,128)(2,1)S(1)}, bf16[29,16,128]{2,1,0:T(8,128)(2,1)S(1)}, u32[]{:S(2)}, u32[]{:S(2)}) %collective-permute-start.1) | collective-permute-done | bytes 118816 | tf_op jit(solution)/shard_map/ppermute | solution.py:547
  23.0 2.5 %shard_map.56 = (f32[88,16,128]{2,1,0:T(8,128)S(1)}, f32[88,16,128]{2,1,0:T(8,128)S(1)}, bf16[23,16,128]{2,1,0:T(8,128)(2,1)S(1)}, bf16[23,16,128]{2,1,0:T(8,128)(2,1)S(1)}) custom-call(f32[1024,128]{1,0:T(8,128)S(1)} %bitcast.7, s32[1024,128]{1,0:T(8,128)S(1)} %bitcast.10, f32[16,128]{1,0:T(8,128)S(1)} %broadcast_in_dim.2.own_map, ...), custom_call_target="tpu_custom_call" | custom-call | tf_op jit(solution)/shard_map/pallas_call | solution.py:581
  25.5 0.0 copy-start.4
  25.5 0.9 %copy-done.4 = f32[88,16,128]{2,1,0:T(8,128)} copy-done((f32[88,16,128]{2,1,0:T(8,128)}, f32[88,16,128]{2,1,0:T(8,128)S(1)}, u32[]{:S(2)}) %copy-start.4) | copy-done | bytes 720920
  26.3 3.6 %collective-permute-start.3 = (bf16[23,16,128]{2,1,0:T(8,128)(2,1)S(1)}, bf16[23,16,128]{2,1,0:T(8,128)(2,1)S(1)}, u32[]{:S(2)}, u32[]{:S(2)}) collective-permute-start(bf16[23,16,128]{2,1,0:T(8,128)(2,1)S(1)} %get-tuple-element.21.own_side), channel_id=1, source_target_pairs={{1,0},{2,1},{3,2},{4,3},{5,4},{6,5},{7,6},{9,8},{10,9},{11,10},{12... | collective-permute-start | bytes 282632 | tf_op jit(solution)/shard_map/ppermute | solution.py:547
  29.9 3.2 %collective-permute-start.2 = (bf16[23,16,128]{2,1,0:T(8,128)(2,1)S(1)}, bf16[23,16,128]{2,1,0:T(8,128)(2,1)S(1)}, u32[]{:S(2)}, u32[]{:S(2)}) collective-permute-start(bf16[23,16,128]{2,1,0:T(8,128)(2,1)S(1)} %get-tuple-element.20), channel_id=1, source_target_pairs={{0,1},{1,2},{2,3},{3,4},{4,5},{5,6},{6,7},{8,9},{9,10},{10,11},{11... | collective-permute-start | bytes 282632 | tf_op jit(solution)/shard_map/ppermute | solution.py:547
  33.1 0.3 collective-permute-done.3.from_right
  33.4 1.3 %collective-permute-done.2.from_left = bf16[23,16,128]{2,1,0:T(8,128)(2,1)S(1)} collective-permute-done((bf16[23,16,128]{2,1,0:T(8,128)(2,1)S(1)}, bf16[23,16,128]{2,1,0:T(8,128)(2,1)S(1)}, u32[]{:S(2)}, u32[]{:S(2)}) %collective-permute-start.2) | collective-permute-done | bytes 94240 | tf_op jit(solution)/shard_map/ppermute | solution.py:547
  34.7 0.0 copy-start.6
  34.7 0.7 %copy-done.6 = f32[2]{0:T(128)S(1)} copy-done((f32[2]{0:T(128)S(1)}, f32[2]{0:T(128)}, u32[]{:S(2)}) %copy-start.6) | copy-done | bytes 32
  35.4 3.7 %shard_map.57 = (f32[88,16,128]{2,1,0:T(8,128)S(1)}, f32[88,16,128]{2,1,0:T(8,128)S(1)}, f32[88,16,128]{2,1,0:T(8,128)S(1)}, f32[88,16,128]{2,1,0:T(8,128)S(1)}, s32[24,128]{1,0:T(8,128)S(1)}) custom-call(f32[2]{0:T(128)S(1)} %copy-done.6, f32[88,16,128]{2,1,0:T(8,128)S(1)} %get-tuple-element.18.pa, f32[88,16,128]{2,1,0:T(8,128)} %copy-done.4, ...), custom_call_target="tpu_custom_call" | custom-call | tf_op jit(solution)/shard_map/pallas_call | solution.py:587
  39.0 0.0 copy-start.2
  39.0 0.9 %copy-done.2 = f32[88,16,128]{2,1,0:T(8,128)} copy-done((f32[88,16,128]{2,1,0:T(8,128)}, f32[88,16,128]{2,1,0:T(8,128)S(1)}, u32[]{:S(2)}) %copy-start.2) | copy-done | bytes 720920
  39.9 0.0 all-to-all-done.got
  39.9 0.0 copy-start.3
  39.9 1.1 %copy-done.3 = f32[88,16,128]{2,1,0:T(8,128)S(1)} copy-done((f32[88,16,128]{2,1,0:T(8,128)S(1)}, f32[88,16,128]{2,1,0:T(8,128)}, u32[]{:S(2)}) %copy-start.3) | copy-done | bytes 720920
  41.0 17.3 %shard_map.59 = f32[1024,128]{1,0:T(8,128)} custom-call(s32[24,128]{1,0:T(8,128)S(1)} %get-tuple-element.22.maps, bf16[32,72,128]{2,1,0:T(8,128)(2,1)S(1)} %all-to-all-done.got, f32[88,16,128]{2,1,0:T(8,128)S(1)} %get-tuple-element.23.we, f32[88,16,128]{2,1,0:T(8,128)S(1)} %get-tuple-element.24.wo, f32[88,16,128]{2,1,0:T(8,128)S(1)} %get-tuple-element.25.ce, ...), custom_call_target="tpu_custom_call" | custom-call | tf_op jit(solution)/shard_map/pallas_call | solution.py:595
  (3 shorter events, 0.0 us)
Async XLA Ops:
  0.0 0.9 %copy-start.5 = (bf16[1,32,4096]{2,1,0:T(8,128)(2,1)S(1)}, bf16[1,32,4096]{2,1,0:T(8,128)(2,1)}, u32[]{:S(2)}) copy-start(bf16[1,32,4096]{2,1,0:T(8,128)(2,1)} %param.8) | copy-start | bytes 786436
  3.3 7.1 %copy-start.7 = (s32[32,1]{0,1:T(1,128)S(1)}, s32[32,1]{0,1:T(1,128)}, u32[]{:S(2)}) copy-start(s32[32,1]{0,1:T(1,128)} %param.9) | copy-start | bytes 388
  3.3 7.2 %copy-start = (f32[16,64,128]{2,1,0:T(8,128)S(1)}, f32[16,64,128]{2,1,0:T(8,128)}, u32[]{:S(2)}) copy-start(f32[16,64,128]{2,1,0:T(8,128)} %param.5) | copy-start | bytes 1572868
  3.3 7.2 %copy-start.1 = (s32[16,64,128]{2,1,0:T(8,128)S(1)}, s32[16,64,128]{2,1,0:T(8,128)}, u32[]{:S(2)}) copy-start(s32[16,64,128]{2,1,0:T(8,128)} %param.6) | copy-start | bytes 1572868
  3.3 36.6 %all-to-all-start = ((bf16[32,72,128]{2,1,0:T(8,128)(2,1)}), bf16[32,72,128]{2,1,0:T(8,128)(2,1)S(1)}, u32[]{:S(2)}, u32[]{:S(2)}) async-start(bf16[32,72,128]{2,1,0:T(8,128)(2,1)} %shard_map.58), calls=%async_computation | async-start | bytes 1179648 | tf_op jit(solution)/shard_map/all_to_all | solution.py:568
  10.7 6.9 %collective-permute-start = (bf16[29,16,128]{2,1,0:T(8,128)(2,1)S(1)}, bf16[29,16,128]{2,1,0:T(8,128)(2,1)S(1)}, u32[]{:S(2)}, u32[]{:S(2)}) collective-permute-start(bf16[29,16,128]{2,1,0:T(8,128)(2,1)S(1)} %get-tuple-element.16), channel_id=1, source_target_pairs={{0,8},{8,16},{16,24},{1,9},{9,17},{17,25},{2,10},{10,18},{18,26},{... | collective-permute-start | bytes 356360 | tf_op jit(solution)/shard_map/ppermute | solution.py:547
  14.0 9.0 %collective-permute-start.1 = (bf16[29,16,128]{2,1,0:T(8,128)(2,1)S(1)}, bf16[29,16,128]{2,1,0:T(8,128)(2,1)S(1)}, u32[]{:S(2)}, u32[]{:S(2)}) collective-permute-start(bf16[29,16,128]{2,1,0:T(8,128)(2,1)S(1)} %get-tuple-element.17), channel_id=1, source_target_pairs={{8,0},{16,8},{24,16},{9,1},{17,9},{25,17},{10,2},{18,10},{26,18},{... | collective-permute-start | bytes 356360 | tf_op jit(solution)/shard_map/ppermute | solution.py:547
  25.5 0.9 %copy-start.4 = (f32[88,16,128]{2,1,0:T(8,128)}, f32[88,16,128]{2,1,0:T(8,128)S(1)}, u32[]{:S(2)}) copy-start(f32[88,16,128]{2,1,0:T(8,128)S(1)} %get-tuple-element.19.la) | copy-start | bytes 2162692
  26.3 7.1 %collective-permute-start.3 = (bf16[23,16,128]{2,1,0:T(8,128)(2,1)S(1)}, bf16[23,16,128]{2,1,0:T(8,128)(2,1)S(1)}, u32[]{:S(2)}, u32[]{:S(2)}) collective-permute-start(bf16[23,16,128]{2,1,0:T(8,128)(2,1)S(1)} %get-tuple-element.21.own_side), channel_id=1, source_target_pairs={{1,0},{2,1},{3,2},{4,3},{5,4},{6,5},{7,6},{9,8},{10,9},{11,10},{12... | collective-permute-start | bytes 282632 | tf_op jit(solution)/shard_map/ppermute | solution.py:547
  29.9 4.8 %collective-permute-start.2 = (bf16[23,16,128]{2,1,0:T(8,128)(2,1)S(1)}, bf16[23,16,128]{2,1,0:T(8,128)(2,1)S(1)}, u32[]{:S(2)}, u32[]{:S(2)}) collective-permute-start(bf16[23,16,128]{2,1,0:T(8,128)(2,1)S(1)} %get-tuple-element.20), channel_id=1, source_target_pairs={{0,1},{1,2},{2,3},{3,4},{4,5},{5,6},{6,7},{8,9},{9,10},{10,11},{11... | collective-permute-start | bytes 282632 | tf_op jit(solution)/shard_map/ppermute | solution.py:547
  34.7 0.7 %copy-start.6 = (f32[2]{0:T(128)S(1)}, f32[2]{0:T(128)}, u32[]{:S(2)}) copy-start(f32[2]{0:T(128)} %volts.1) | copy-start | bytes 28
  39.0 0.9 %copy-start.2 = (f32[88,16,128]{2,1,0:T(8,128)}, f32[88,16,128]{2,1,0:T(8,128)S(1)}, u32[]{:S(2)}) copy-start(f32[88,16,128]{2,1,0:T(8,128)S(1)} %get-tuple-element.26.co) | copy-start | bytes 2162692
  39.9 1.1 %copy-start.3 = (f32[88,16,128]{2,1,0:T(8,128)S(1)}, f32[88,16,128]{2,1,0:T(8,128)}, u32[]{:S(2)}) copy-start(f32[88,16,128]{2,1,0:T(8,128)} %copy-done.2) | copy-start | bytes 2162692

commit v2 on v1

--- a/solution.py
+++ b/solution.py
@@ -8,6 +8,8 @@
 from jax.sharding import PartitionSpec as P
 
 HALO = 12
+JOIN = 20
+TALL = 40
 debye_term = 1.0
 damping = 0.5
 
@@ -28,79 +30,107 @@
     return value if shift == 0 else pltpu.roll(value, shift, 1)
 
 
-def x_pack_kernel(nz, rx, pot, lab, own_map, up, down):
-    def row(ref, x):
-        return ref[pl.ds(x, nz, stride=rx), :]
-
-    for out, first, near in ((up, 0, 0), (down, rx - HALO, rx - 4)):
+def is_even(axis):
+    return lax.rem(lax.axis_index(axis), 2) == 0
+
+
+def chunked(low, high, most, fn):
+    count = -(-(high - low) // most)
+    size = -(-(high - low) // count)
+    if count == 1:
+        fn(low, size)
+        return
+
+    def body(step, carry):
+        fn(jnp.minimum(low + step * size, high - size), size)
+        return carry
+
+    lax.fori_loop(0, count, body, 0)
+
+
+def x_pack_kernel(nz, rx, pot, lab, own_map, one, two):
+    even = is_even("gx")
+    for out, is_last in ((one, even), (two, jnp.logical_not(even))):
+        base = jnp.where(is_last, rx - HALO, 0)
+        near = jnp.where(is_last, HALO - 4, 0)
+
+        def row(ref, x):
+            return ref[pl.ds(x, nz, stride=rx), :]
+
         for i in range(HALO):
-            value = row(pot, first + i)
-            high = value.astype(bf16)
-            out[i] = high
-            offset = first + i - near
-            if 0 <= offset < 4:
-                out[HALO + offset] = (value - high.astype(f32)).astype(bf16)
-            out[HALO + 4 + i] = (row(lab, first + i) + 1).astype(f32).astype(bf16)
-        out[2 * HALO + 4] = own_map[...].astype(bf16)
-
-
-def y_pack_kernel(nz, rx, pot, lab, own_map, before, after, pa, la, left, right):
-    wide = rx + 2 * HALO
-    for i in range(HALO):
-        value = before[i].astype(f32)
-        if i >= HALO - 4:
-            value = value + before[HALO + i - (HALO - 4)].astype(f32)
-        pa[i] = value
-        la[i] = before[HALO + 4 + i].astype(f32)
-        value = after[i].astype(f32)
-        if i < 4:
-            value = value + after[HALO + i].astype(f32)
-        pa[HALO + rx + i] = value
-        la[HALO + rx + i] = after[HALO + 4 + i].astype(f32)
-
-    def copy_rows(step, carry):
-        for q in range(4):
-            x = step * 4 + q
-            pa[HALO + x] = pot[pl.ds(x, nz, stride=rx), :]
-            la[HALO + x] = (lab[pl.ds(x, nz, stride=rx), :] + 1).astype(f32)
-        return carry
-
-    lax.fori_loop(0, rx // 4, copy_rows, 0)
-
+            out[i] = row(pot, base + i).astype(bf16)
+            out[HALO + 4 + i] = (row(lab, base + i) + 1).astype(f32).astype(bf16)
+        for i in range(4):
+            value = row(pot, base + near + i)
+            out[HALO + i] = (value - value.astype(bf16).astype(f32)).astype(bf16)
+        out[2 * HALO + 4] = own_map[pl.ds(0, nz), :].astype(bf16)
+
+
+def strip_groups(nz, pa, la, one, two, first, size):
     lane = lane_iota(nz)
     is_low = between(lane, 12, 16)
     is_label = lane >= 16
     group_of = lane // 32
-
-    def group(g):
+    even = is_even("gy")
+    for g in range(size):
         to_left = jnp.zeros((nz, 128), f32)
         to_right = jnp.zeros((nz, 128), f32)
         for q in range(4):
-            value = pa[g * 4 + q]
-            code = la[g * 4 + q]
+            value = pa[(first + g) * 4 + q]
+            code = la[(first + g) * 4 + q]
             high = value.astype(bf16).astype(f32)
             low = value - high
-            one = jnp.where(is_label, roll(code, 16), jnp.where(is_low, roll(low, 12), high))
-            two = jnp.where(is_label, roll(code, 28), jnp.where(is_low, roll(low, 16), roll(high, 12)))
+            left = jnp.where(is_label, roll(code, 16), jnp.where(is_low, roll(low, 12), high))
+            right = jnp.where(is_label, roll(code, 28), jnp.where(is_low, roll(low, 16), roll(high, 12)))
             here = group_of == q
-            to_left = jnp.where(here, roll(one, 32 * q), to_left)
-            to_right = jnp.where(here, roll(two, 32 * q), to_right)
-        left[g] = to_left.astype(bf16)
-        right[g] = to_right.astype(bf16)
-
-    def groups(first, size):
+            to_left = jnp.where(here, roll(left, 32 * q), to_left)
+            to_right = jnp.where(here, roll(right, 32 * q), to_right)
+        one[first + g] = jnp.where(even, to_right, to_left).astype(bf16)
+        two[first + g] = jnp.where(even, to_left, to_right).astype(bf16)
+
+
+def y_own_kernel(nz, rx, pot, lab, pa, la, one, two):
+    def copy_rows(first, size):
         for k in range(size):
-            group(first + k)
-
-    chunked(0, wide // 4, 4, groups)
+            x = first + k
+            pa[HALO + x] = pot[pl.ds(x, nz, stride=rx), :]
+            la[HALO + x] = (lab[pl.ds(x, nz, stride=rx), :] + 1).astype(f32)
+
+    chunked(0, rx, 16, copy_rows)
+    chunked(
+        HALO // 4, (HALO + rx) // 4, 4, lambda first, size: strip_groups(nz, pa, la, one, two, first, size)
+    )
+
+
+def y_edge_kernel(nz, rx, own_map, got_one, got_two, *refs):
+    pa, la, one, two = refs[4:]
+    wide = rx + 2 * HALO
+    even = is_even("gx")
+
+    def before(i):
+        return jnp.where(even, got_two[i].astype(f32), got_one[i].astype(f32))
+
+    def after(i):
+        return jnp.where(even, got_one[i].astype(f32), got_two[i].astype(f32))
+
+    for i in range(HALO):
+        value = before(i)
+        if i >= HALO - 4:
+            value = value + before(HALO + i - (HALO - 4))
+        pa[i] = value
+        la[i] = before(HALO + 4 + i)
+        value = after(i)
+        if i < 4:
+            value = value + after(HALO + i)
+        pa[HALO + rx + i] = value
+        la[HALO + rx + i] = after(HALO + 4 + i)
+    strip_groups(nz, pa, la, one, two, 0, HALO // 4)
+    strip_groups(nz, pa, la, one, two, (HALO + rx) // 4, HALO // 4)
     row = lax.broadcasted_iota(jnp.int32, (nz, 128), 0)
-    maps = jnp.where(
-        row == 0,
-        before[2 * HALO + 4].astype(f32),
-        jnp.where(row == 1, own_map[...], after[2 * HALO + 4].astype(f32)),
-    ).astype(bf16)
-    left[wide // 4] = maps
-    right[wide // 4] = maps
+    last = 2 * HALO + 4
+    maps = jnp.where(row == 0, before(last), jnp.where(row == 1, own_map[pl.ds(0, nz), :], after(last)))
+    one[wide // 4] = maps.astype(bf16)
+    two[wide // 4] = maps.astype(bf16)
 
 
 NOWHERE = -1000
@@ -165,20 +195,6 @@
         ref[:, pl.ds(8 + nz, 8), :] = zero
 
 
-def chunked(low, high, most, fn):
-    count = -(-(high - low) // most)
-    size = -(-(high - low) // count)
-    if count == 1:
-        fn(low, size)
-        return
-
-    def body(step, carry):
-        fn(jnp.minimum(low + step * size, high - size), size)
-        return carry
-
-    lax.fori_loop(0, count, body, 0)
-
-
 def absent(place):
     index = lax.axis_index("gy")
     none_before = between(place, 148, 169) & (index == 0)
@@ -186,7 +202,8 @@
     return none_before | none_after
 
 
-def weight_kernel(nz, rx, volts, pa, la, from_left, from_right, own_side, we, wo, ce, co, maps, ppe, ppo, lbe, lbo):
+def weight_kernel(nz, rx, own_map, pa, la, got_one, got_two, own_side, wc, maps, ppe, ppo, lbe, lbo):
+    we, wo, ce, co = (wc.at[k] for k in range(4))
     wide = rx + 2 * HALO
     groups = wide // 4
     clear_pads((ppe, ppo), wide, nz)
@@ -212,8 +229,11 @@
         return jnp.concatenate(pieces, axis=0)
 
     flat = (groups * nz, 128)
-    left = from_left[pl.ds(0, groups)].reshape(flat)
-    right = from_right[pl.ds(0, groups)].reshape(flat)
+    even = is_even("gy")
+    swapped_one = got_one[pl.ds(0, groups)].reshape(flat)
+    swapped_two = got_two[pl.ds(0, groups)].reshape(flat)
+    left = jnp.where(even, swapped_two, swapped_one)
+    right = jnp.where(even, swapped_one, swapped_two)
     for q in range(4):
         value = pa[pl.ds(q, groups, stride=4)].reshape(flat)
         high, middle, low = parts_of(value)
@@ -235,8 +255,8 @@
         place = 2 * lane + t
         keep = (place < 136) | between(place, 149, 168) | between(place, 184, 203) | (place >= 248)
         kept.append(keep & ~absent(place))
-    v0 = volts[0]
-    v1 = volts[1]
+    v0 = jnp.broadcast_to(own_map[pl.ds(16, 1), :], (nz, 128))
+    v1 = jnp.broadcast_to(own_map[pl.ds(17, 1), :], (nz, 128))
 
     def rows(first, size):
         for k in range(size):
@@ -258,13 +278,28 @@
     for i in (0, wide - 1):
         for ref in (we, wo, ce, co):
             ref[i] = zero
-    for at, ref in ((0, from_left), (8, own_side), (16, from_right)):
-        maps[pl.ds(at, 8), :] = ref[groups].astype(f32)[0:8].astype(jnp.int32)
-
-
-def slot_kernel(count, ny, tiles, blocks, out, field):
+    map_one, map_two = got_one[groups].astype(f32)[0:8], got_two[groups].astype(f32)[0:8]
+    maps[pl.ds(0, 8), :] = jnp.where(even, map_two, map_one).astype(jnp.int32)
+    maps[pl.ds(8, 8), :] = own_side[groups].astype(f32)[0:8].astype(jnp.int32)
+    maps[pl.ds(16, 8), :] = jnp.where(even, map_one, map_two).astype(jnp.int32)
+
+
+def slot_kernel(count, ny, tiles, blocks_in, owners_in, volts_in, pot_in, lab_in, slots, own, pot, lab, *scratch):
+    field, blocks, out, owners, volts, in_sems, out_sems = scratch
     rows = tiles * 8
+    pairs = [(owners_in, owners), (volts_in, volts), (pot_in, pot), (lab_in, lab)]
+    copies = [pltpu.make_async_copy(*pair, in_sems.at[4 + k]) for k, pair in enumerate(pairs)]
+    width = rows * 128 // 4
+    columns = [pl.ds(k * width, width) for k in range(4)]
+    block_copies = [
+        pltpu.make_async_copy(blocks_in.at[:, part], blocks.at[:, part], in_sems.at[k]) for k, part in enumerate(columns)
+    ]
+    for copy in block_copies + copies:
+        copy.start()
+    own[...] = jnp.zeros(own.shape, f32)
     for r in range(rows):
+        if r % (rows // 4) == 0:
+            block_copies[r // (rows // 4)].wait()
         field[pl.ds(r, count, stride=rows), :] = blocks[:, pl.ds(r * 128, 128)].astype(f32)
     lane = lane_iota(8)
     sub = lax.broadcasted_iota(jnp.int32, (8, 128), 0)
@@ -297,20 +332,31 @@
         out[k] = jnp.concatenate(parts, axis=0).astype(bf16)
         return carry
 
-    def some(step, carry):
-        for k in range(4):
-            one(step * 4 + k, carry)
-        return carry
-
-    lax.fori_loop(0, count // 4, some, 0)
-
-
-def sweep_kernel(nz, rx, count, tiles, maps, got, we, wo, ce, co, pot, out, *scratch):
-    (re, ro, xe, xo, ye, yo, ue, uo, cut_e, cut_o, ch_a, ch_l, ch_r, ve, vo) = scratch
+    part = count // 4
+    out_copies = []
+    for step in range(4):
+        chunked(step * part, (step + 1) * part, 8, lambda first, size: [one(first + k, 0) for k in range(size)])
+        span = pl.ds(step * part, part)
+        out_copies.append(pltpu.make_async_copy(out.at[span], slots.at[span], out_sems.at[step]))
+        out_copies[-1].start()
+    for copy in copies:
+        copy.wait()
+    own[pl.ds(0, 16), pl.ds(0, count)] = jnp.broadcast_to(owners[...].astype(f32), (16, count))
+    for k in (0, 1):
+        own[pl.ds(16 + k, 1), :] = jnp.full((1, 128), volts[k], f32)
+    for copy in out_copies:
+        copy.wait()
+
+
+def sweep_kernel(nz, rx, count, tiles, maps_in, got, wc, pot, out, *scratch):
+    (re, ro, xe, xo, ye, yo, ue, uo, cut_e, cut_o, ch_a, ch_s, ve, vo, maps, map_sem) = scratch
+    map_copy = pltpu.make_async_copy(maps_in, maps, map_sem)
+    map_copy.start()
+    we, wo, ce, co = (wc.at[k] for k in range(4))
     rhs, xs, ys, us, cuts = (re, ro), (xe, xo), (ye, yo), (ue, uo), (cut_e, cut_o)
     weights, charged, couplings = (we, wo), (ve, vo), (ce, co)
     wide = rx + 2 * HALO
-    tall = rx + 32
+    tall = rx + TALL
     per_plane = rx // (8 * tiles)
     lane = lane_iota(nz)
     index_x, index_y = lax.axis_index("gx"), lax.axis_index("gy")
@@ -318,6 +364,8 @@
     has_low, has_high = jnp.where(low_x, 1.0, 0.0), jnp.where(high_x, 1.0, 0.0)
     clear_pads(rhs + xs + ys + us, wide, nz)
     clear_pads(cuts, cut_e.shape[0], nz)
+
+    low_lanes, high_lanes = lane_iota(8) < 16, lane_iota(8) >= 16
 
     def place(p):
         slot = got[p].astype(f32)
@@ -333,8 +381,12 @@
             ok = depth * 8 * tiles < HALO
             return jnp.where(ok, z, nz), part, jnp.where(ok, depth, 0)
 
-        def put(ref, z, row, value):
-            ref[pl.ds(pl.multiple_of(z * tall + row, 8), 8), :] = value
+        def put(ref, z, row, value, mask=None):
+            target = pl.ds(pl.multiple_of(z * tall + row, 8), 8)
+            if mask is None:
+                ref[target, :] = value
+            else:
+                pltpu.store(ref.at[target, :], value, mask=mask)
 
         z, part, _ = where_to(9, 0)
         for t in range(tiles):
@@ -357,25 +409,18 @@
         zr, part_r, _ = where_to(17, 0)
         for t in range(tiles):
             value = roll(sides, -32 * t)
-            put(ch_l, zl, 16 + (part_l * tiles + t) * 8, value)
-            put(ch_r, zr, 16 + (part_r * tiles + t) * 8, value)
+            put(ch_s, zl, 16 + (part_l * tiles + t) * 8, value, low_lanes)
+            put(ch_s, zr, 16 + (part_r * tiles + t) * 8, value, high_lanes)
         for at, side in ((0, 1), (32, -1)):
             value = roll(corners, -at)
             second = None if tiles == 1 else roll(corners, -at - 64)
-            for which, ref in ((1 + side, ch_l), (17 + side, ch_r)):
+            for which, lanes in ((1 + side, low_lanes), (17 + side, high_lanes)):
                 z, _, depth = where_to(which, side)
                 if tiles == 1:
-                    put(ref, z, (16 + rx + depth * 8) if side > 0 else (8 - depth * 8), value)
+                    put(ch_s, z, (16 + rx + depth * 8) if side > 0 else (8 - depth * 8), value, lanes)
                 else:
-                    put(ref, z, (16 + rx) if side > 0 else 8, value)
-                    put(ref, z, (24 + rx) if side > 0 else 0, second)
-
-    def place_some(step, carry):
-        for k in range(8):
-            place(step * 8 + k)
-        return carry
-
-    lax.fori_loop(0, count // 8, place_some, 0)
+                    put(ch_s, z, (16 + rx) if side > 0 else 8, value, lanes)
+                    put(ch_s, z, (24 + rx) if side > 0 else 0, second, lanes)
 
     row, column = grid_of(256, 256)
     cell = cell_of(place_of(column))
@@ -388,8 +433,11 @@
     gather = jnp.where((source == cell) & (cell != NOWHERE), damping, 0.0).astype(bf16)
     row, column = grid_of(256, 128)
     final = ones_where(cell_of(place_of(row)) == column)
-    is_low = (lane < HALO) & (index_y > 0)
-    is_high = between(lane, 16, 16 + HALO) & (index_y < lax.axis_size("gy") - 1)
+    is_strip = (lane < HALO) & (index_y > 0)
+    is_strip = is_strip | (between(lane, 16, 16 + HALO) & (index_y < lax.axis_size("gy") - 1))
+
+    map_copy.wait()
+    chunked(0, count, 8, lambda first, size: [place(first + p) for p in range(size)])
 
     def add_charge(present):
         def rows(first, size):
@@ -397,9 +445,7 @@
             for k in range(size):
                 x = first + k + 4
                 a = ch_a[pl.ds(x, nz, stride=tall), :]
-                low = ch_l[pl.ds(x, nz, stride=tall), :]
-                high = ch_r[pl.ds(x, nz, stride=tall), :]
-                strip = jnp.where(is_low, low, jnp.where(is_high, high, 0.0))
+                strip = jnp.where(is_strip, ch_s[pl.ds(x, nz, stride=tall), :], 0.0)
                 if present is not None:
                     a = jnp.where(present, a, 0.0)
                     strip = jnp.where(present, strip, 0.0)
@@ -416,7 +462,7 @@
         return rows
 
     chunked(1, HALO, HALO, add_charge(low_x))
-    chunked(HALO, HALO + rx, 16, add_charge(None))
+    chunked(HALO, HALO + rx, 32, add_charge(None))
     chunked(HALO + rx, wide - 1, HALO, add_charge(high_x))
 
     def iterate(src, dst, low, high):
@@ -427,7 +473,7 @@
                 for t in (0, 1):
                     dst[t][i, pl.ds(8, nz), :] = read(rhs[t], i, nz) + couplings[t][i] * near[t]
 
-        chunked(low, high, 28, rows)
+        chunked(low, high, 42, rows)
 
     def cut(level, at, edge, step):
         starts = {2: 0, 3: 1, 4: 3}
@@ -459,7 +505,7 @@
                         shared = jnp.where(ghosts[t], 0.0, near[t])
                         rhs[t][i, pl.ds(8, nz), :] = held + couplings[t][i] * shared
 
-            chunked(lowest, wide - lowest, 28, residual)
+            chunked(lowest, wide - lowest, 42, residual)
         iterate(rhs, xs, lowest + 1, wide - lowest - 1)
         iterate(xs, ys, lowest + 2, wide - lowest - 2)
         some = ends if sweep == 0 else ends[:2]
@@ -504,9 +550,11 @@
                     + jnp.where(keep, us[t][pl.ds(first, size), pl.ds(8, nz), :].reshape(flat), 0.0)
                     for t in (0, 1)
                 ]
-            parts = parts_of(jnp.concatenate(both, axis=1))
+            whole = jnp.concatenate(both, axis=1)
+            high = whole.astype(bf16)
+            rest = (whole - high.astype(f32)).astype(bf16)
             matrix = final if last else gather
-            total = product(parts[2], matrix) + product(parts[1], matrix) + product(parts[0], matrix)
+            total = product(rest, matrix) + product(high, matrix)
             if last:
                 for k in range(size):
                     x = first + k - HALO
@@ -518,8 +566,8 @@
                     value = value + us[t][pl.ds(first, size), pl.ds(8, nz), :]
                 us[t][pl.ds(first, size), pl.ds(8, nz), :] = value
 
-        for first in range(low, high, 16):
-            join(first, min(16, high - first))
+        for first in range(low, high, JOIN):
+            join(first, min(JOIN, high - first))
 
 
 def vmem():
@@ -530,21 +578,31 @@
     return pl.BlockSpec(memory_space=pltpu.SMEM)
 
 
-def call(kernel, ins, outs, scratch=()):
+def hbm():
+    return pl.BlockSpec(memory_space=pltpu.HBM)
+
+
+def anywhere():
+    return pl.BlockSpec(memory_space=pl.ANY)
+
+
+def call(kernel, ins, outs, scratch=(), aliases=(), room=8):
     return pl.pallas_call(
         kernel,
         in_specs=ins,
         out_specs=jax.tree.map(lambda _: vmem(), outs),
         out_shape=outs,
         scratch_shapes=list(scratch),
-        compiler_params=pltpu.CompilerParams(vmem_limit_bytes=50 << 20),
-    )
-
-
-def shifted(value, axis, steps):
-    count = lax.axis_size(axis)
-    first, last = max(0, -steps), min(count, count - steps)
-    return lax.ppermute(value, axis, [(source, source + steps) for source in range(first, last)])
+        input_output_aliases=dict(aliases),
+        compiler_params=pltpu.CompilerParams(vmem_limit_bytes=room << 20),
+    )
+
+
+def swapped(value, axis, first):
+    pairs = []
+    for low in range(first, lax.axis_size(axis) - 1, 2):
+        pairs += [(low, low + 1), (low + 1, low)]
+    return lax.ppermute(value, axis, pairs)
 
 
 def on_device(potential, labels, voltages, ion_blocks, owner_map):
@@ -554,50 +612,75 @@
     count, cells = blocks.shape
     tiles = cells // (8 * ry)
     sds = jax.ShapeDtypeStruct
+    ny = lax.axis_size("gy")
+
+    slot_rows = 8 * (tiles + (2 if tiles == 1 else 3) + 2)
+    slot_shape = (count, slot_rows, ry)
+    brick = (nz, rx, ry)
+    slots, own_map, potential, labels = pl.pallas_call(
+        functools.partial(slot_kernel, count, ny, tiles),
+        in_specs=[hbm()] * 5,
+        out_specs=(hbm(), vmem(), vmem(), vmem()),
+        out_shape=(sds(slot_shape, bf16), sds((24, ry), f32), sds(brick, f32), sds(brick, jnp.int32)),
+        scratch_shapes=[
+            pltpu.VMEM((count * tiles * 8, 128), f32),
+            pltpu.VMEM((count, cells), bf16),
+            pltpu.VMEM(slot_shape, bf16),
+            pltpu.VMEM((1, count), jnp.int32),
+            pltpu.SMEM((2,), f32),
+            pltpu.SemaphoreType.DMA((8,)),
+            pltpu.SemaphoreType.DMA((4,)),
+        ],
+        compiler_params=pltpu.CompilerParams(vmem_limit_bytes=12 << 20),
+    )(*(pltpu.with_memory_space_constraint(v, pltpu.HBM) for v in (blocks, owner_map.reshape(1, count), voltages, potential, labels)))
     pot = potential.reshape(nz * rx, ry)
     lab = labels.reshape(nz * rx, ry)
-    ny = lax.axis_size("gy")
-
-    slot_rows = 8 * (tiles + (2 if tiles == 1 else 3) + 2)
-    slots = call(
-        functools.partial(slot_kernel, count, ny, tiles),
-        [vmem()],
-        sds((count, slot_rows, ry), bf16),
-        [pltpu.VMEM((count * tiles * 8, 128), f32)],
-    )(blocks)
+
+    strip = sds((2 * HALO + 5, nz, ry), bf16)
+    one, two = call(
+        functools.partial(x_pack_kernel, nz, rx),
+        [vmem()] * 3,
+        (strip, strip),
+    )(pot, lab, own_map)
+    one = swapped(one, "gx", 0)
+    two = swapped(two, "gx", 1)
+
     got = lax.all_to_all(slots, ("gx", "gy"), split_axis=0, concat_axis=0, tiled=True)
 
-    own_map = jnp.broadcast_to(
-        jnp.pad(owner_map[:, 0].astype(f32), (0, 128 - count))[None], (nz, 128)
-    )
-    strip = sds((2 * HALO + 5, nz, ry), bf16)
-    up, down = call(functools.partial(x_pack_kernel, nz, rx), [vmem()] * 3, (strip, strip))(
-        pot, lab, own_map
-    )
-    before = shifted(down, "gx", 1)
-    after = shifted(up, "gx", -1)
     field = sds((wide, nz, ry), f32)
     side = sds((wide // 4 + 1, nz, ry), bf16)
+    packed = (field, field, side, side)
+    pa, la, left, right = call(functools.partial(y_own_kernel, nz, rx), [vmem()] * 2, packed)(pot, lab)
     pa, la, left, right = call(
-        functools.partial(y_pack_kernel, nz, rx), [vmem()] * 5, (field, field, side, side)
-    )(pot, lab, own_map, before, after)
-    from_left = shifted(right, "gy", 1)
-    from_right = shifted(left, "gy", -1)
+        functools.partial(y_edge_kernel, nz, rx), [vmem()] * 7, packed, (), {3: 0, 4: 1, 5: 2, 6: 3}
+    )(own_map, one, two, pa, la, left, right)
+    got_one = swapped(left, "gy", 0)
+    got_two = swapped(right, "gy", 1)
     padded = pltpu.VMEM((wide, nz + 16, 128), f32)
-    we, wo, ce, co, maps = call(
+    wc, maps = call(
         functools.partial(weight_kernel, nz, rx),
-        [smem()] + [vmem()] * 5,
-        (field, field, field, field, sds((24, 128), jnp.int32)),
-        [padded, padded] + [pltpu.VMEM((wide, nz, 128), f32)] * 2,
-    )(voltages, pa, la, from_left, from_right, left)
+        [vmem()] * 6,
+        (sds((4, wide, nz, ry), f32), sds((24, 128), jnp.int32)),
+        [padded, padded]
+        + [pltpu.VMEM((wide, nz, 128), f32)] * 2,
+        room=16,
+    )(own_map, pa, la, got_one, got_two, left)
     cuts = pltpu.VMEM((24, nz + 16, 128), f32)
-    plane = pltpu.VMEM(((nz + 1) * (rx + 32), 128), f32)
+    plane = pltpu.VMEM(((nz + 1) * (rx + TALL), 128), f32)
     out = call(
         functools.partial(sweep_kernel, nz, rx, count, tiles),
-        [smem()] + [vmem()] * 6,
+        [anywhere()] + [vmem()] * 3,
         sds((nz * rx, ry), f32),
-        [padded] * 8 + [cuts, cuts] + [plane] * 3 + [pltpu.VMEM((wide, nz, 128), f32)] * 2,
-    )(maps, got, we, wo, ce, co, pot)
+        [padded] * 8
+        + [cuts, cuts]
+        + [plane] * 2
+        + [pltpu.VMEM((wide, nz, 128), f32)] * 2
+        + [
+            pltpu.SMEM((24, 128), jnp.int32),
+            pltpu.SemaphoreType.DMA,
+        ],
+        room=20,
+    )(maps, got, wc, pot)
     return out.reshape(nz, rx, ry)
 
 

time: 58.6 us -> 46.7 us (0.80)
  the two profiles are of different devices: /device:TPU:1 before, /device:TPU:19 now
where the time goes in v2:
time: 46.7 us; the launch traced here: 46.5 us
  Pallas kernels  22.6 us (48%)
  starting transfers between devices  15.1 us (32%)
  waiting for transfers between devices  8.67 us (19%)
    pallas_call x1, Pallas kernels, on_device(): call(functools.partial(sweep_kernel, nz, rx, count, tiles), [anywhere()]...  15 us
    ppermute x4, starting transfers between devices, swapped(): return lax.ppermute(value, axis, pairs)  8.79 us
    ppermute x4, waiting for transfers between devices, swapped(): return lax.ppermute(value, axis, pairs)  8.67 us
    all_to_all x1, starting transfers between devices, on_device(): lax.all_to_all(slots, ('gx', 'gy'), split_axis=0, concat_axis=0, tiled=True)  6.28 us
    pallas_call x1, Pallas kernels, on_device(): call(functools.partial(weight_kernel, nz, rx), [vmem()] * 6, (sds((4, wid...  2.55 us
    pallas_call x1, Pallas kernels, on_device(): pl.pallas_call(functools.partial(slot_kernel, count, ny, tiles), in_specs...  2.39 us
    pallas_call x1, Pallas kernels, on_device(): call(functools.partial(y_own_kernel, nz, rx), [vmem()] * 2, packed)  1.8 us
  transfers between devices with their start and end apart: 5, of which 3 were waited for; matrix products, arithmetic and copies ran while one was open for 0% of the time, Pallas kernels for 11%

profile of v2, /device:TPU:19, one launch (start us, length us, event | category | flops | bytes accessed | tf_op | source)
XLA Modules:
  0.0 46.5 jit_solution(12003389658955878500)
XLA Ops:
  0.0 2.4 %shard_map.55 = (bf16[32,72,128]{2,1,0:T(8,128)(2,1)}, f32[24,128]{1,0:T(8,128)S(1)}, f32[16,64,128]{2,1,0:T(8,128)S(1)}, s32[16,64,128]{2,1,0:T(8,128)S(1)}) custom-call(bf16[32,4096]{1,0:T(8,128)(2,1)} %bitcast.10, s32[1,32]{1,0:T(1,128)} %bitcast.11, f32[2]{0:T(128)} %volts_in.1, f32[16,64,128]{2,1,0:T(8,128)} %pot_in.1, s32[16,64,128]{2,1,0:T(8,128)} %lab_in.1), custom_call_target="tpu_custom_call" | custom-call | tf_op jit(solution)/shard_map/pallas_call | solution.py:620
  2.4 6.3 %all-to-all-start = ((bf16[32,72,128]{2,1,0:T(8,128)(2,1)}), bf16[32,72,128]{2,1,0:T(8,128)(2,1)}, u32[]{:S(2)}, u32[]{:S(2)}) async-start(bf16[32,72,128]{2,1,0:T(8,128)(2,1)} %get-tuple-element.35), calls=%async_computation | async-start | bytes 1179648 | tf_op jit(solution)/shard_map/all_to_all | solution.py:648
  8.7 0.3 shard_map.56
  9.0 0.3 collective-permute-start
  9.3 4.0 %collective-permute-start.1 = (bf16[29,16,128]{2,1,0:T(8,128)(2,1)S(1)}, bf16[29,16,128]{2,1,0:T(8,128)(2,1)S(1)}, u32[]{:S(2)}, u32[]{:S(2)}) collective-permute-start(bf16[29,16,128]{2,1,0:T(8,128)(2,1)S(1)} %get-tuple-element.25), channel_id=1, source_target_pairs={{8,16},{16,8},{9,17},{17,9},{10,18},{18,10},{11,19},{19,11},{12,20... | collective-permute-start | bytes 356360 | tf_op jit(solution)/shard_map/ppermute | solution.py:605
  13.3 1.8 %shard_map.57 = (f32[88,16,128]{2,1,0:T(8,128)S(1)}, f32[88,16,128]{2,1,0:T(8,128)S(1)}, bf16[23,16,128]{2,1,0:T(8,128)(2,1)S(1)}, bf16[23,16,128]{2,1,0:T(8,128)(2,1)S(1)}) custom-call(f32[1024,128]{1,0:T(8,128)S(1)} %bitcast.6, s32[1024,128]{1,0:T(8,128)S(1)} %bitcast.9), custom_call_target="tpu_custom_call" | custom-call | tf_op jit(solution)/shard_map/pallas_call | solution.py:653
  15.1 2.1 %collective-permute-done.got_one = bf16[29,16,128]{2,1,0:T(8,128)(2,1)S(1)} collective-permute-done((bf16[29,16,128]{2,1,0:T(8,128)(2,1)S(1)}, bf16[29,16,128]{2,1,0:T(8,128)(2,1)S(1)}, u32[]{:S(2)}, u32[]{:S(2)}) %collective-permute-start) | collective-permute-done | bytes 118816 | tf_op jit(solution)/shard_map/ppermute | solution.py:605
  17.3 4.4 %collective-permute-done.1.got_two = bf16[29,16,128]{2,1,0:T(8,128)(2,1)S(1)} collective-permute-done((bf16[29,16,128]{2,1,0:T(8,128)(2,1)S(1)}, bf16[29,16,128]{2,1,0:T(8,128)(2,1)S(1)}, u32[]{:S(2)}, u32[]{:S(2)}) %collective-permute-start.1) | collective-permute-done | bytes 118816 | tf_op jit(solution)/shard_map/ppermute | solution.py:605
  21.6 0.6 %shard_map.58 = (f32[88,16,128]{2,1,0:T(8,128)S(1)}, f32[88,16,128]{2,1,0:T(8,128)S(1)}, bf16[23,16,128]{2,1,0:T(8,128)(2,1)S(1)}, bf16[23,16,128]{2,1,0:T(8,128)(2,1)S(1)}) custom-call(f32[24,128]{1,0:T(8,128)S(1)} %get-tuple-element.21.own_map, ...), custom_call_target="tpu_custom_call", output_to_operand_aliasing={{0}: (3, {}), {1}: (4, {}), {2}: (5, {}), {3}: (6, {})} | custom-call | tf_op jit(solution)/shard_map/pallas_call | solution.py:654
  22.3 4.4 %collective-permute-start.3 = (bf16[23,16,128]{2,1,0:T(8,128)(2,1)S(1)}, bf16[23,16,128]{2,1,0:T(8,128)(2,1)S(1)}, u32[]{:S(2)}, u32[]{:S(2)}) collective-permute-start(bf16[23,16,128]{2,1,0:T(8,128)(2,1)S(1)} %get-tuple-element.33), channel_id=1, source_target_pairs={{1,2},{2,1},{3,4},{4,3},{5,6},{6,5},{9,10},{10,9},{11,12},{12,11},... | collective-permute-start | bytes 282632 | tf_op jit(solution)/shard_map/ppermute | solution.py:605
  26.6 0.1 collective-permute-start.2
  26.7 2.2 %collective-permute-done.3.got_two = bf16[23,16,128]{2,1,0:T(8,128)(2,1)S(1)} collective-permute-done((bf16[23,16,128]{2,1,0:T(8,128)(2,1)S(1)}, bf16[23,16,128]{2,1,0:T(8,128)(2,1)S(1)}, u32[]{:S(2)}, u32[]{:S(2)}) %collective-permute-start.3) | collective-permute-done | bytes 94240 | tf_op jit(solution)/shard_map/ppermute | solution.py:605
  28.9 0.0 collective-permute-done.2.got_one
  28.9 2.6 %shard_map.59 = (f32[4,88,16,128]{3,2,1,0:T(8,128)S(1)}, s32[24,128]{1,0:T(8,128)S(1)}) custom-call(f32[24,128]{1,0:T(8,128)S(1)} %get-tuple-element.21.own_map, f32[88,16,128]{2,1,0:T(8,128)S(1)} %get-tuple-element.30.pa, f32[88,16,128]{2,1,0:T(8,128)S(1)} %get-tuple-element.31.la, bf16[23,16,128]{2,1,0:T(8,128)(2,1)S(1)} %collective-permute-done.2.got_one, ...), custom_call_target="tpu_custom_call" | custom-call | tf_op jit(solution)/shard_map/pallas_call | solution.py:660
  31.4 0.0 all-to-all-done.got
  31.4 15.0 %shard_map.60 = f32[1024,128]{1,0:T(8,128)} custom-call(s32[24,128]{1,0:T(8,128)S(1)} %get-tuple-element.34.maps_in, bf16[32,72,128]{2,1,0:T(8,128)(2,1)} %all-to-all-done.got, f32[4,88,16,128]{3,2,1,0:T(8,128)S(1)} %get-tuple-element.36.wc, f32[1024,128]{1,0:T(8,128)S(1)} %bitcast.7), custom_call_target="tpu_custom_call" | custom-call | tf_op jit(solution)/shard_map/pallas_call | solution.py:670
Async XLA Ops:
  2.4 29.0 %all-to-all-start = ((bf16[32,72,128]{2,1,0:T(8,128)(2,1)}), bf16[32,72,128]{2,1,0:T(8,128)(2,1)}, u32[]{:S(2)}, u32[]{:S(2)}) async-start(bf16[32,72,128]{2,1,0:T(8,128)(2,1)} %get-tuple-element.35), calls=%async_computation | async-start | bytes 1179648 | tf_op jit(solution)/shard_map/all_to_all | solution.py:648
  9.0 8.3 %collective-permute-start = (bf16[29,16,128]{2,1,0:T(8,128)(2,1)S(1)}, bf16[29,16,128]{2,1,0:T(8,128)(2,1)S(1)}, u32[]{:S(2)}, u32[]{:S(2)}) collective-permute-start(bf16[29,16,128]{2,1,0:T(8,128)(2,1)S(1)} %get-tuple-element.24), channel_id=1, source_target_pairs={{0,8},{8,0},{16,24},{24,16},{1,9},{9,1},{17,25},{25,17},{2,10},{10... | collective-permute-start | bytes 356360 | tf_op jit(solution)/shard_map/ppermute | solution.py:605
  9.3 12.3 %collective-permute-start.1 = (bf16[29,16,128]{2,1,0:T(8,128)(2,1)S(1)}, bf16[29,16,128]{2,1,0:T(8,128)(2,1)S(1)}, u32[]{:S(2)}, u32[]{:S(2)}) collective-permute-start(bf16[29,16,128]{2,1,0:T(8,128)(2,1)S(1)} %get-tuple-element.25), channel_id=1, source_target_pairs={{8,16},{16,8},{9,17},{17,9},{10,18},{18,10},{11,19},{19,11},{12,20... | collective-permute-start | bytes 356360 | tf_op jit(solution)/shard_map/ppermute | solution.py:605
  22.3 6.6 %collective-permute-start.3 = (bf16[23,16,128]{2,1,0:T(8,128)(2,1)S(1)}, bf16[23,16,128]{2,1,0:T(8,128)(2,1)S(1)}, u32[]{:S(2)}, u32[]{:S(2)}) collective-permute-start(bf16[23,16,128]{2,1,0:T(8,128)(2,1)S(1)} %get-tuple-element.33), channel_id=1, source_target_pairs={{1,2},{2,1},{3,4},{4,3},{5,6},{6,5},{9,10},{10,9},{11,12},{12,11},... | collective-permute-start | bytes 282632 | tf_op jit(solution)/shard_map/ppermute | solution.py:605
  26.6 2.2 %collective-permute-start.2 = (bf16[23,16,128]{2,1,0:T(8,128)(2,1)S(1)}, bf16[23,16,128]{2,1,0:T(8,128)(2,1)S(1)}, u32[]{:S(2)}, u32[]{:S(2)}) collective-permute-start(bf16[23,16,128]{2,1,0:T(8,128)(2,1)S(1)} %get-tuple-element.32.own_side), channel_id=1, source_target_pairs={{0,1},{1,0},{2,3},{3,2},{4,5},{5,4},{6,7},{7,6},{8,9},{9,8},{10,11... | collective-permute-start | bytes 282632 | tf_op jit(solution)/shard_map/ppermute | solution.py:605

commit v3 on v2

--- a/solution.py
+++ b/solution.py
@@ -8,7 +8,7 @@
 from jax.sharding import PartitionSpec as P
 
 HALO = 12
-JOIN = 20
+JOIN = 40
 TALL = 40
 debye_term = 1.0
 damping = 0.5
@@ -96,7 +96,7 @@
             pa[HALO + x] = pot[pl.ds(x, nz, stride=rx), :]
             la[HALO + x] = (lab[pl.ds(x, nz, stride=rx), :] + 1).astype(f32)
 
-    chunked(0, rx, 16, copy_rows)
+    chunked(0, rx, 64, copy_rows)
     chunked(
         HALO // 4, (HALO + rx) // 4, 4, lambda first, size: strip_groups(nz, pa, la, one, two, first, size)
     )
@@ -202,7 +202,7 @@
     return none_before | none_after
 
 
-def weight_kernel(nz, rx, own_map, pa, la, got_one, got_two, own_side, wc, maps, ppe, ppo, lbe, lbo):
+def weight_kernel(nz, rx, tiles, own_map, pa, la, got_one, got_two, own_side, wc, maps, ppe, ppo, lbe, lbo):
     we, wo, ce, co = (wc.at[k] for k in range(4))
     wide = rx + 2 * HALO
     groups = wide // 4
@@ -273,15 +273,25 @@
                 w_out[i] = jnp.where(code > 0.5, w, 0.0)
                 c_out[i] = jnp.where(plasma, inverse, 0.0)
 
-    chunked(1, wide - 1, 22, rows)
+    chunked(1, wide - 1, 86, rows)
     zero = jnp.zeros((nz, 128), f32)
     for i in (0, wide - 1):
         for ref in (we, wo, ce, co):
             ref[i] = zero
     map_one, map_two = got_one[groups].astype(f32)[0:8], got_two[groups].astype(f32)[0:8]
-    maps[pl.ds(0, 8), :] = jnp.where(even, map_two, map_one).astype(jnp.int32)
-    maps[pl.ds(8, 8), :] = own_side[groups].astype(f32)[0:8].astype(jnp.int32)
-    maps[pl.ds(16, 8), :] = jnp.where(even, map_one, map_two).astype(jnp.int32)
+    all_maps = (jnp.where(even, map_two, map_one), own_side[groups].astype(f32)[0:8], jnp.where(even, map_one, map_two))
+    per_plane = rx // (8 * tiles)
+    tall = rx + TALL
+    row = lax.broadcasted_iota(jnp.int32, (8, 128), 0)
+    for k, index in enumerate(all_maps):
+        z = jnp.floor((index + 0.5) / per_plane)
+        part = index - z * per_plane
+        depth = jnp.where(row == 2, part, per_plane - 1 - part)
+        beside = jnp.where(depth * (8 * tiles) < HALO, z, float(nz)) * tall
+        depth = jnp.where(depth * (8 * tiles) < HALO, depth, 0.0) * 8
+        inner = z * tall + 16 + part * (8 * tiles)
+        target = jnp.where(row == 1, inner, jnp.where(row == 0, beside + 8 - depth, beside + 16 + rx + depth))
+        maps[pl.ds(8 * k, 8), :] = target.astype(jnp.int32)
 
 
 def slot_kernel(count, ny, tiles, blocks_in, owners_in, volts_in, pot_in, lab_in, slots, own, pot, lab, *scratch):
@@ -300,14 +310,14 @@
     for r in range(rows):
         if r % (rows // 4) == 0:
             block_copies[r // (rows // 4)].wait()
-        field[pl.ds(r, count, stride=rows), :] = blocks[:, pl.ds(r * 128, 128)].astype(f32)
+        field[pl.ds(r, count, stride=rows + 8), :] = blocks[:, pl.ds(r * 128, 128)].astype(f32)
     lane = lane_iota(8)
     sub = lax.broadcasted_iota(jnp.int32, (8, 128), 0)
 
     def one(k, carry):
         def tile(offset, t):
             brick = lax.rem(k + offset + count, count)
-            return field[pl.ds(pl.multiple_of(brick * rows + t * 8, 8), 8), :]
+            return field[pl.ds(pl.multiple_of(brick * (rows + 8) + t * 8, 8), 8), :]
 
         parts = [tile(0, t) for t in range(tiles)]
         if tiles == 1:
@@ -317,9 +327,7 @@
             parts += [tile(ny, 0), mixed, tile(-ny, tiles - 1)]
 
         def pair(offset, t, at):
-            low = roll(tile(offset - 1, t), 12 + at)
-            high = roll(tile(offset + 1, t), 16 + at)
-            return jnp.where(between(lane, at, at + 12), low, high)
+            return roll(jnp.where(lane < 64, tile(offset + 1, t), tile(offset - 1, t)), HALO + at)
 
         sides = jnp.zeros((8, 128), f32)
         for t in range(tiles):
@@ -348,16 +356,21 @@
         copy.wait()
 
 
-def sweep_kernel(nz, rx, count, tiles, maps_in, got, wc, pot, out, *scratch):
-    (re, ro, xe, xo, ye, yo, ue, uo, cut_e, cut_o, ch_a, ch_s, ve, vo, maps, map_sem) = scratch
+def sweep_kernel(nz, rx, count, tiles, maps_in, got_in, wc, pot, out_hbm, *scratch):
+    (re, ro, xe, xo, ye, yo, ue, uo, cut_e, cut_o, ch_a, ch_s, ve, vo, maps, got, out, map_sem, sems, out_sems) = scratch
     map_copy = pltpu.make_async_copy(maps_in, maps, map_sem)
     map_copy.start()
+    some = count // 4
+    got_copies = []
+    for k in range(4):
+        span = pl.ds(k * some, some)
+        got_copies.append(pltpu.make_async_copy(got_in.at[span], got.at[span], sems.at[k]))
+        got_copies[k].start()
     we, wo, ce, co = (wc.at[k] for k in range(4))
     rhs, xs, ys, us, cuts = (re, ro), (xe, xo), (ye, yo), (ue, uo), (cut_e, cut_o)
     weights, charged, couplings = (we, wo), (ve, vo), (ce, co)
     wide = rx + 2 * HALO
     tall = rx + TALL
-    per_plane = rx // (8 * tiles)
     lane = lane_iota(nz)
     index_x, index_y = lax.axis_index("gx"), lax.axis_index("gy")
     low_x, high_x = index_x > 0, index_x < lax.axis_size("gx") - 1
@@ -365,79 +378,63 @@
     clear_pads(rhs + xs + ys + us, wide, nz)
     clear_pads(cuts, cut_e.shape[0], nz)
 
-    low_lanes, high_lanes = lane_iota(8) < 16, lane_iota(8) >= 16
+    low_lanes, high_lanes = lane_iota(8) < HALO, lane_iota(8) >= HALO
 
     def place(p):
         slot = got[p].astype(f32)
         pieces = [slot[8 * t : 8 * t + 8] for t in range(slot.shape[0] // 8)]
 
-        def where_to(which, side):
-            index = maps[which, p]
-            z = index // per_plane
-            part = index - z * per_plane
-            if side == 0:
-                return z, part, None
-            depth = part if side > 0 else per_plane - 1 - part
-            ok = depth * 8 * tiles < HALO
-            return jnp.where(ok, z, nz), part, jnp.where(ok, depth, 0)
-
-        def put(ref, z, row, value, mask=None):
-            target = pl.ds(pl.multiple_of(z * tall + row, 8), 8)
+        def put(ref, row, value, mask=None):
+            target = pl.ds(pl.multiple_of(row, 8), 8)
             if mask is None:
                 ref[target, :] = value
             else:
                 pltpu.store(ref.at[target, :], value, mask=mask)
 
-        z, part, _ = where_to(9, 0)
+        first = maps[9, p]
         for t in range(tiles):
-            put(ch_a, z, 16 + (part * tiles + t) * 8, pieces[t])
-        zp, _, dp = where_to(10, 1)
-        zm, _, dm = where_to(8, -1)
+            put(ch_a, first + t * 8, pieces[t])
+        after, before = maps[10, p], maps[8, p]
+        put(ch_a, after, pieces[tiles])
         if tiles == 1:
-            put(ch_a, zp, 16 + rx + dp * 8, pieces[1])
-            put(ch_a, zm, 8 - dm * 8, pieces[2])
-            next_piece = 3
+            put(ch_a, before, pieces[2])
         else:
-            put(ch_a, zp, 16 + rx, pieces[tiles])
-            put(ch_a, zp, 24 + rx, pieces[tiles + 1])
-            put(ch_a, zm, 0, pieces[tiles + 1])
-            put(ch_a, zm, 8, pieces[tiles + 2])
-            next_piece = tiles + 3
-        sides = pieces[next_piece]
-        corners = pieces[next_piece + 1]
-        zl, part_l, _ = where_to(1, 0)
-        zr, part_r, _ = where_to(17, 0)
+            put(ch_a, after + 8, pieces[tiles + 1])
+            put(ch_a, before - 8, pieces[tiles + 1])
+            put(ch_a, before, pieces[tiles + 2])
+        sides, corners = pieces[-2:]
+        low_side, high_side = maps[1, p], maps[17, p]
         for t in range(tiles):
             value = roll(sides, -32 * t)
-            put(ch_s, zl, 16 + (part_l * tiles + t) * 8, value, low_lanes)
-            put(ch_s, zr, 16 + (part_r * tiles + t) * 8, value, high_lanes)
-        for at, side in ((0, 1), (32, -1)):
+            put(ch_s, low_side + t * 8, value, low_lanes)
+            put(ch_s, high_side + t * 8, value, high_lanes)
+        for at, step in ((0, 1), (32, -1)):
             value = roll(corners, -at)
             second = None if tiles == 1 else roll(corners, -at - 64)
-            for which, lanes in ((1 + side, low_lanes), (17 + side, high_lanes)):
-                z, _, depth = where_to(which, side)
-                if tiles == 1:
-                    put(ch_s, z, (16 + rx + depth * 8) if side > 0 else (8 - depth * 8), value, lanes)
-                else:
-                    put(ch_s, z, (16 + rx) if side > 0 else 8, value, lanes)
-                    put(ch_s, z, (24 + rx) if side > 0 else 0, second, lanes)
+            for which, lanes in ((1 + step, low_lanes), (17 + step, high_lanes)):
+                target = maps[which, p]
+                put(ch_s, target, value, lanes)
+                if tiles > 1:
+                    put(ch_s, target + 8 * step, second, lanes)
 
     row, column = grid_of(256, 256)
     cell = cell_of(place_of(column))
     spread = ones_where(
         ((row < 128) & (row == cell))
         | (between(row, 128, 128 + HALO) & (row - (128 + HALO) == cell))
-        | (between(row, 144, 144 + HALO) & (row - 16 == cell))
+        | (between(row, 128 + HALO, 128 + 2 * HALO) & (row - HALO == cell))
     )
     source = cell_of(place_of(row))
     gather = jnp.where((source == cell) & (cell != NOWHERE), damping, 0.0).astype(bf16)
     row, column = grid_of(256, 128)
     final = ones_where(cell_of(place_of(row)) == column)
     is_strip = (lane < HALO) & (index_y > 0)
-    is_strip = is_strip | (between(lane, 16, 16 + HALO) & (index_y < lax.axis_size("gy") - 1))
+    is_strip = is_strip | (between(lane, HALO, 2 * HALO) & (index_y < lax.axis_size("gy") - 1))
 
     map_copy.wait()
-    chunked(0, count, 8, lambda first, size: [place(first + p) for p in range(size)])
+    for k in range(4):
+        got_copies[k].wait()
+        chunked(k * some, (k + 1) * some, 8, lambda first, size: [place(first + p) for p in range(size)])
 
     def add_charge(present):
         def rows(first, size):
@@ -462,7 +459,7 @@
         return rows
 
     chunked(1, HALO, HALO, add_charge(low_x))
-    chunked(HALO, HALO + rx, 32, add_charge(None))
+    chunked(HALO, HALO + rx, 64, add_charge(None))
     chunked(HALO + rx, wide - 1, HALO, add_charge(high_x))
 
     def iterate(src, dst, low, high):
@@ -473,7 +470,7 @@
                 for t in (0, 1):
                     dst[t][i, pl.ds(8, nz), :] = read(rhs[t], i, nz) + couplings[t][i] * near[t]
 
-        chunked(low, high, 42, rows)
+        chunked(low, high, 84, rows)
 
     def cut(level, at, edge, step):
         starts = {2: 0, 3: 1, 4: 3}
@@ -491,6 +488,7 @@
     ends = [(0, HALO + 7, -1), (6, HALO + rx - 8, 1), (12, HALO - 8, 1), (18, HALO + rx + 7, -1)]
     ghosts = [(2 * lane + t == 168) | (2 * lane + t == 183) | absent(2 * lane + t) for t in (0, 1)]
     own = lane < 64
+    out_copies = []
     for sweep in range(3):
         last = sweep == 2
         lowest = 1 + 4 * sweep
@@ -505,15 +503,12 @@
                         shared = jnp.where(ghosts[t], 0.0, near[t])
                         rhs[t][i, pl.ds(8, nz), :] = held + couplings[t][i] * shared
 
-            chunked(lowest, wide - lowest, 42, residual)
-        iterate(rhs, xs, lowest + 1, wide - lowest - 1)
-        iterate(xs, ys, lowest + 2, wide - lowest - 2)
-        some = ends if sweep == 0 else ends[:2]
-        for level in (2, 3, 4):
-            for at, edge, step in some:
+            chunked(lowest, wide - lowest, 84, residual)
+        low, high = lowest + 3, wide - lowest - 3
+        for level, src, dst in ((2, rhs, xs), (3, xs, ys), (4, ys, xs)):
+            for at, edge, step in ends if sweep == 0 else ends[:2]:
                 cut(level, at, edge, step)
-        low, high = lowest + 3, wide - lowest - 3
-        iterate(ys, xs, low, high)
+            iterate(src, dst, lowest + level - 1, wide - lowest - level + 1)
 
         def scale(first, end, factor):
             for i in range(first, end):
@@ -559,6 +554,12 @@
                 for k in range(size):
                     x = first + k - HALO
                     out[pl.ds(x, nz, stride=rx), :] = total[k * nz : (k + 1) * nz] + pot[pl.ds(x, nz, stride=rx), :]
+                span = pl.ds(first - HALO, size)
+                copy = pltpu.make_async_copy(
+                    out.reshape(nz, rx, 128).at[:, span], out_hbm.at[:, span], out_sems.at[len(out_copies)]
+                )
+                copy.start()
+                out_copies.append(copy)
                 return
             for t in (0, 1):
                 value = total[:, 128 * t : 128 * t + 128].reshape(size, nz, 128)
@@ -566,8 +567,11 @@
                     value = value + us[t][pl.ds(first, size), pl.ds(8, nz), :]
                 us[t][pl.ds(first, size), pl.ds(8, nz), :] = value
 
-        for first in range(low, high, JOIN):
-            join(first, min(JOIN, high - first))
+        step = 32 if last else JOIN
+        for first in range(low, high, step):
+            join(first, min(step, high - first))
+    for copy in out_copies:
+        copy.wait()
 
 
 def vmem():
@@ -623,7 +627,7 @@
         out_specs=(hbm(), vmem(), vmem(), vmem()),
         out_shape=(sds(slot_shape, bf16), sds((24, ry), f32), sds(brick, f32), sds(brick, jnp.int32)),
         scratch_shapes=[
-            pltpu.VMEM((count * tiles * 8, 128), f32),
+            pltpu.VMEM((count * (tiles + 1) * 8, 128), f32),
             pltpu.VMEM((count, cells), bf16),
             pltpu.VMEM(slot_shape, bf16),
             pltpu.VMEM((1, count), jnp.int32),
@@ -658,7 +662,7 @@
     got_two = swapped(right, "gy", 1)
     padded = pltpu.VMEM((wide, nz + 16, 128), f32)
     wc, maps = call(
-        functools.partial(weight_kernel, nz, rx),
+        functools.partial(weight_kernel, nz, rx, tiles),
         [vmem()] * 6,
         (sds((4, wide, nz, ry), f32), sds((24, 128), jnp.int32)),
         [padded, padded]
@@ -667,21 +671,25 @@
     )(own_map, pa, la, got_one, got_two, left)
     cuts = pltpu.VMEM((24, nz + 16, 128), f32)
     plane = pltpu.VMEM(((nz + 1) * (rx + TALL), 128), f32)
-    out = call(
+    return pl.pallas_call(
         functools.partial(sweep_kernel, nz, rx, count, tiles),
-        [anywhere()] + [vmem()] * 3,
-        sds((nz * rx, ry), f32),
-        [padded] * 8
+        in_specs=[anywhere(), hbm(), vmem(), vmem()],
+        out_specs=hbm(),
+        out_shape=sds(brick, f32),
+        scratch_shapes=[padded] * 8
         + [cuts, cuts]
         + [plane] * 2
         + [pltpu.VMEM((wide, nz, 128), f32)] * 2
         + [
             pltpu.SMEM((24, 128), jnp.int32),
+            pltpu.VMEM(slot_shape, bf16),
+            pltpu.VMEM((nz * rx, ry), f32),
             pltpu.SemaphoreType.DMA,
+            pltpu.SemaphoreType.DMA((4,)),
+            pltpu.SemaphoreType.DMA((-(-rx // 16),)),
         ],
-        room=20,
-    )(maps, got, wc, pot)
-    return out.reshape(nz, rx, ry)
+        compiler_params=pltpu.CompilerParams(vmem_limit_bytes=24 << 20),
+    )(maps, pltpu.with_memory_space_constraint(got, pltpu.HBM), wc, pot)
 
 
 def solution(mesh):

time: 46.7 us -> 40.7 us (0.87)
  Pallas kernels: 22.6 us -> 16.5 us
    pallas_call x2, Pallas kernels: 17.6 us -> 11.8 us  [the longest x1 9.54 us: on_device(): pl.pallas_call(functools.partial(sweep_kernel, nz, rx, count, tiles), in_...]
  transfers between devices with their start and end apart: 5 -> 5, of which waited for: 3 -> 3; matrix products, arithmetic and copies ran while one was open for 0% -> 0% of each run, Pallas kernels for 11% -> 12%
where the time goes in v3:
time: 40.7 us; the launch traced here: 40.5 us
  Pallas kernels  16.5 us (41%)
  starting transfers between devices  15.2 us (37%)
  waiting for transfers between devices  8.52 us (21%)
    pallas_call x1, Pallas kernels, on_device(): pl.pallas_call(functools.partial(sweep_kernel, nz, rx, count, tiles), in_...  9.54 us
    ppermute x4, starting transfers between devices, swapped(): return lax.ppermute(value, axis, pairs)  8.97 us
    ppermute x4, waiting for transfers between devices, swapped(): return lax.ppermute(value, axis, pairs)  8.52 us
    all_to_all x1, starting transfers between devices, on_device(): lax.all_to_all(slots, ('gx', 'gy'), split_axis=0, concat_axis=0, tiled=True)  6.28 us
    pallas_call x1, Pallas kernels, on_device(): call(functools.partial(weight_kernel, nz, rx, tiles), [vmem()] * 6, (sds(...  2.31 us
    pallas_call x1, Pallas kernels, on_device(): pl.pallas_call(functools.partial(slot_kernel, count, ny, tiles), in_specs...  1.99 us
    pallas_call x1, Pallas kernels, on_device(): call(functools.partial(y_own_kernel, nz, rx), [vmem()] * 2, packed)  1.76 us
  transfers between devices with their start and end apart: 5, of which 3 were waited for; matrix products, arithmetic and copies ran while one was open for 0% of the time, Pallas kernels for 12%

profile of v3, /device:TPU:19, one launch (start us, length us, event | category | flops | bytes accessed | tf_op | source)
XLA Modules:
  0.0 40.5 jit_solution(3658163426632300714)
XLA Ops:
  0.0 2.0 %shard_map.55 = (bf16[32,72,128]{2,1,0:T(8,128)(2,1)}, f32[24,128]{1,0:T(8,128)S(1)}, f32[16,64,128]{2,1,0:T(8,128)S(1)}, s32[16,64,128]{2,1,0:T(8,128)S(1)}) custom-call(bf16[32,4096]{1,0:T(8,128)(2,1)} %bitcast.9, s32[1,32]{1,0:T(1,128)} %bitcast.10, f32[2]{0:T(128)} %volts_in.1, f32[16,64,128]{2,1,0:T(8,128)} %pot_in.1, s32[16,64,128]{2,1,0:T(8,128)} %lab_in.1), custom_call_target="tpu_custom_call" | custom-call | tf_op jit(solution)/shard_map/pallas_call | solution.py:624
  2.0 6.3 %all-to-all-start = ((bf16[32,72,128]{2,1,0:T(8,128)(2,1)}), bf16[32,72,128]{2,1,0:T(8,128)(2,1)}, u32[]{:S(2)}, u32[]{:S(2)}) async-start(bf16[32,72,128]{2,1,0:T(8,128)(2,1)} %get-tuple-element.35), calls=%async_computation | async-start | bytes 1179648 | tf_op jit(solution)/shard_map/all_to_all | solution.py:652
  8.3 0.3 shard_map.56
  8.6 0.3 collective-permute-start
  8.9 4.0 %collective-permute-start.1 = (bf16[29,16,128]{2,1,0:T(8,128)(2,1)S(1)}, bf16[29,16,128]{2,1,0:T(8,128)(2,1)S(1)}, u32[]{:S(2)}, u32[]{:S(2)}) collective-permute-start(bf16[29,16,128]{2,1,0:T(8,128)(2,1)S(1)} %get-tuple-element.25), channel_id=1, source_target_pairs={{8,16},{16,8},{9,17},{17,9},{10,18},{18,10},{11,19},{19,11},{12,20... | collective-permute-start | bytes 356360 | tf_op jit(solution)/shard_map/ppermute | solution.py:609
  12.9 1.8 %shard_map.57 = (f32[88,16,128]{2,1,0:T(8,128)S(1)}, f32[88,16,128]{2,1,0:T(8,128)S(1)}, bf16[23,16,128]{2,1,0:T(8,128)(2,1)S(1)}, bf16[23,16,128]{2,1,0:T(8,128)(2,1)S(1)}) custom-call(f32[1024,128]{1,0:T(8,128)S(1)} %bitcast.5, s32[1024,128]{1,0:T(8,128)S(1)} %bitcast.8), custom_call_target="tpu_custom_call" | custom-call | tf_op jit(solution)/shard_map/pallas_call | solution.py:657
  14.7 2.2 %collective-permute-done.got_one = bf16[29,16,128]{2,1,0:T(8,128)(2,1)S(1)} collective-permute-done((bf16[29,16,128]{2,1,0:T(8,128)(2,1)S(1)}, bf16[29,16,128]{2,1,0:T(8,128)(2,1)S(1)}, u32[]{:S(2)}, u32[]{:S(2)}) %collective-permute-start) | collective-permute-done | bytes 118816 | tf_op jit(solution)/shard_map/ppermute | solution.py:609
  16.9 4.4 %collective-permute-done.1.got_two = bf16[29,16,128]{2,1,0:T(8,128)(2,1)S(1)} collective-permute-done((bf16[29,16,128]{2,1,0:T(8,128)(2,1)S(1)}, bf16[29,16,128]{2,1,0:T(8,128)(2,1)S(1)}, u32[]{:S(2)}, u32[]{:S(2)}) %collective-permute-start.1) | collective-permute-done | bytes 118816 | tf_op jit(solution)/shard_map/ppermute | solution.py:609
  21.2 0.6 %shard_map.58 = (f32[88,16,128]{2,1,0:T(8,128)S(1)}, f32[88,16,128]{2,1,0:T(8,128)S(1)}, bf16[23,16,128]{2,1,0:T(8,128)(2,1)S(1)}, bf16[23,16,128]{2,1,0:T(8,128)(2,1)S(1)}) custom-call(f32[24,128]{1,0:T(8,128)S(1)} %get-tuple-element.21.own_map, ...), custom_call_target="tpu_custom_call", output_to_operand_aliasing={{0}: (3, {}), {1}: (4, {}), {2}: (5, {}), {3}: (6, {})} | custom-call | tf_op jit(solution)/shard_map/pallas_call | solution.py:658
  21.9 4.5 %collective-permute-start.3 = (bf16[23,16,128]{2,1,0:T(8,128)(2,1)S(1)}, bf16[23,16,128]{2,1,0:T(8,128)(2,1)S(1)}, u32[]{:S(2)}, u32[]{:S(2)}) collective-permute-start(bf16[23,16,128]{2,1,0:T(8,128)(2,1)S(1)} %get-tuple-element.33), channel_id=1, source_target_pairs={{1,2},{2,1},{3,4},{4,3},{5,6},{6,5},{9,10},{10,9},{11,12},{12,11},... | collective-permute-start | bytes 282632 | tf_op jit(solution)/shard_map/ppermute | solution.py:609
  26.4 0.1 collective-permute-start.2
  26.5 2.0 %collective-permute-done.3.got_two = bf16[23,16,128]{2,1,0:T(8,128)(2,1)S(1)} collective-permute-done((bf16[23,16,128]{2,1,0:T(8,128)(2,1)S(1)}, bf16[23,16,128]{2,1,0:T(8,128)(2,1)S(1)}, u32[]{:S(2)}, u32[]{:S(2)}) %collective-permute-start.3) | collective-permute-done | bytes 94240 | tf_op jit(solution)/shard_map/ppermute | solution.py:609
  28.5 0.0 collective-permute-done.2.got_one
  28.5 2.3 %shard_map.59 = (f32[4,88,16,128]{3,2,1,0:T(8,128)S(1)}, s32[24,128]{1,0:T(8,128)S(1)}) custom-call(f32[24,128]{1,0:T(8,128)S(1)} %get-tuple-element.21.own_map, f32[88,16,128]{2,1,0:T(8,128)S(1)} %get-tuple-element.30.pa, f32[88,16,128]{2,1,0:T(8,128)S(1)} %get-tuple-element.31.la, bf16[23,16,128]{2,1,0:T(8,128)(2,1)S(1)} %collective-permute-done.2.got_one, ...), custom_call_target="tpu_custom_call" | custom-call | tf_op jit(solution)/shard_map/pallas_call | solution.py:664
  30.8 0.0 all-to-all-done.got_in
  30.8 9.5 %shard_map.60 = f32[16,64,128]{2,1,0:T(8,128)} custom-call(s32[24,128]{1,0:T(8,128)S(1)} %get-tuple-element.34.maps_in, bf16[32,72,128]{2,1,0:T(8,128)(2,1)} %all-to-all-done.got_in, f32[4,88,16,128]{3,2,1,0:T(8,128)S(1)} %get-tuple-element.36.wc, f32[1024,128]{1,0:T(8,128)S(1)} %bitcast.6), custom_call_target="tpu_custom_call" | custom-call | tf_op jit(solution)/shard_map/pallas_call | solution.py:674
Async XLA Ops:
  2.0 28.8 %all-to-all-start = ((bf16[32,72,128]{2,1,0:T(8,128)(2,1)}), bf16[32,72,128]{2,1,0:T(8,128)(2,1)}, u32[]{:S(2)}, u32[]{:S(2)}) async-start(bf16[32,72,128]{2,1,0:T(8,128)(2,1)} %get-tuple-element.35), calls=%async_computation | async-start | bytes 1179648 | tf_op jit(solution)/shard_map/all_to_all | solution.py:652
  8.6 8.3 %collective-permute-start = (bf16[29,16,128]{2,1,0:T(8,128)(2,1)S(1)}, bf16[29,16,128]{2,1,0:T(8,128)(2,1)S(1)}, u32[]{:S(2)}, u32[]{:S(2)}) collective-permute-start(bf16[29,16,128]{2,1,0:T(8,128)(2,1)S(1)} %get-tuple-element.24), channel_id=1, source_target_pairs={{0,8},{8,0},{16,24},{24,16},{1,9},{9,1},{17,25},{25,17},{2,10},{10... | collective-permute-start | bytes 356360 | tf_op jit(solution)/shard_map/ppermute | solution.py:609
  8.9 12.3 %collective-permute-start.1 = (bf16[29,16,128]{2,1,0:T(8,128)(2,1)S(1)}, bf16[29,16,128]{2,1,0:T(8,128)(2,1)S(1)}, u32[]{:S(2)}, u32[]{:S(2)}) collective-permute-start(bf16[29,16,128]{2,1,0:T(8,128)(2,1)S(1)} %get-tuple-element.25), channel_id=1, source_target_pairs={{8,16},{16,8},{9,17},{17,9},{10,18},{18,10},{11,19},{19,11},{12,20... | collective-permute-start | bytes 356360 | tf_op jit(solution)/shard_map/ppermute | solution.py:609
  21.9 6.6 %collective-permute-start.3 = (bf16[23,16,128]{2,1,0:T(8,128)(2,1)S(1)}, bf16[23,16,128]{2,1,0:T(8,128)(2,1)S(1)}, u32[]{:S(2)}, u32[]{:S(2)}) collective-permute-start(bf16[23,16,128]{2,1,0:T(8,128)(2,1)S(1)} %get-tuple-element.33), channel_id=1, source_target_pairs={{1,2},{2,1},{3,4},{4,3},{5,6},{6,5},{9,10},{10,9},{11,12},{12,11},... | collective-permute-start | bytes 282632 | tf_op jit(solution)/shard_map/ppermute | solution.py:609
  26.4 2.1 %collective-permute-start.2 = (bf16[23,16,128]{2,1,0:T(8,128)(2,1)S(1)}, bf16[23,16,128]{2,1,0:T(8,128)(2,1)S(1)}, u32[]{:S(2)}, u32[]{:S(2)}) collective-permute-start(bf16[23,16,128]{2,1,0:T(8,128)(2,1)S(1)} %get-tuple-element.32.own_side), channel_id=1, source_target_pairs={{0,1},{1,0},{2,3},{3,2},{4,5},{5,4},{6,7},{7,6},{8,9},{9,8},{10,11... | collective-permute-start | bytes 282632 | tf_op jit(solution)/shard_map/ppermute | solution.py:609
